TPU v7x, 32 devices: a whole 2x2x4 slice. The times are simulated.
32 devices in a mesh: fsdp: 16 (over z, y, x), tp: 2 (over core).
Axes of the slice: x: 2, y: 2, z: 4, core: 2. Of those that a mesh axis runs over, the one named last changes fastest.
Arguments:
- inputs: bfloat16 [16, 1024, 768], P('fsdp', 'tp'), may hold values from -6 to 6
- query_key_value_weight: bfloat16 [3, 768, 768], P(None, 'fsdp', 'tp'), may hold values from -0.21875 to 0.21875
- attention_out_weight: bfloat16 [768, 768], P('tp', 'fsdp'), may hold values from -3.5 to 3.5
- up_weight: bfloat16 [768, 3072], P('fsdp', 'tp'), may hold values from -0.21875 to 0.21875
- down_weight: bfloat16 [3072, 768], P('tp', 'fsdp'), may hold values from -0.109375 to 0.109375
- qk_bias: bfloat16 [2, 768], P(None, 'fsdp'), may hold values from -3 to 3
- value_bias: bfloat16 [768], P('fsdp'), may hold values from -0.119628906 to 0.119628906
- out_bias: bfloat16 [768], P('fsdp'), may hold values from -1.1953125 to 1.1953125
- ffn_in_bias: bfloat16 [3072], P('fsdp'), may hold values from -3 to 3
- ffn_out_bias: bfloat16 [768], P('fsdp'), may hold values from -1.1953125 to 1.1953125
- norm_gains: bfloat16 [2, 768], P(None, 'fsdp'), may hold values from 0.5 to 1.5
- norm_biases: bfloat16 [2, 768], P(None, 'fsdp'), may hold values from -1.1953125 to 1.1953125
- grad_out: bfloat16 [16, 1024, 768], P('fsdp', 'tp'), may hold values from -6 to 6
Outputs:
- output: bfloat16 [16, 1024, 768], P('fsdp', 'tp')
- grad_input: float32 [16, 1024, 768], P('fsdp', 'tp')
- grad_w_qkv: float32 [3, 768, 768], P(None, 'fsdp', 'tp')
- grad_w_out: float32 [768, 768], P('tp', 'fsdp')
- grad_w_up: float32 [768, 3072], P('fsdp', 'tp')
- grad_w_down: float32 [3072, 768], P('tp', 'fsdp')
- grad_qk_bias: float32 [2, 768], P(None, 'fsdp')
- grad_value_bias: float32 [768], P('fsdp')
- grad_out_bias: float32 [768], P('fsdp')
- grad_ffn_in_bias: float32 [3072], P('fsdp')
- grad_ffn_out_bias: float32 [768], P('fsdp')
- grad_norm_gains: float32 [2, 768], P(None, 'fsdp')
- grad_norm_biases: float32 [2, 768], P(None, 'fsdp')
All inputs are finite; a program needn't handle non-finite values.
Results may differ from a plain program's by a relative error of at most 0.017.
Values may be sent and summed in bfloat16 or wider, within the bound.
A program may use at most 128 MiB of HBM per device.

v0:
```python
from functools import partial

import jax
import jax.numpy as jnp
from jax import lax
from jax.sharding import PartitionSpec as P

HEAD_DIM = 64


norm_eps = 1e-05


def layer_norm(values, gain, shift):
    center = values - jnp.mean(values, -1, keepdims=True)
    spread = jnp.mean(center * center, -1, keepdims=True)
    return center * lax.rsqrt(spread + norm_eps) * gain + shift


def to_heads(merged, head_count):
    lead = merged.shape[:-3]
    seq_count, length, model_cols = merged.shape[-3:]
    split = merged.reshape(lead + (seq_count, length, head_count, model_cols // head_count))
    split = jnp.moveaxis(split, -2, -3)
    return split.reshape(lead + (seq_count * head_count, length, model_cols // head_count))


def from_heads(split, seq_count):
    lead = split.shape[:-3]
    rows_heads, length, head_size = split.shape[-3:]
    head_count = rows_heads // seq_count
    merged = split.reshape(lead + (seq_count, head_count, length, head_size))
    merged = jnp.moveaxis(merged, -3, -2)
    return merged.reshape(lead + (seq_count, length, head_count * head_size))


def causal_block(begin_row, block_rows, end_row):
    rows_at = begin_row + jnp.arange(block_rows)
    cols_at = jnp.arange(end_row)
    return rows_at[:, None] >= cols_at[None, :]


def attend(pieces):
    q_feat, k_feat, values = pieces
    length = q_feat.shape[0]
    block_rows = min(512, length)
    weighted = []
    totals = []
    for begin_row in range(0, length, block_rows):
        end_row = begin_row + block_rows
        scores = jnp.einsum(
            "if,jf->ij",
            q_feat[begin_row:end_row],
            k_feat[:end_row],
            preferred_element_type=jnp.float32,
        )
        scores = jnp.where(causal_block(begin_row, block_rows, end_row), scores, 0.0)
        totals.append(jnp.sum(scores, 1))
        weighted.append(
            jnp.dot(
                scores.astype(jnp.bfloat16), values[:end_row], preferred_element_type=jnp.float32
            )
        )
    return (jnp.concatenate(weighted, 0), jnp.concatenate(totals, 0))


def attend_back(pieces):
    q_feat, k_feat, values, d_weighted, d_totals = pieces
    length, feat_size = k_feat.shape
    block_rows = min(512, length)
    d_query = []
    d_key = jnp.zeros((length, feat_size), jnp.float32)
    d_value = jnp.zeros(values.shape, jnp.float32)
    for begin_row in range(0, length, block_rows):
        end_row = begin_row + block_rows
        causal_mask = causal_block(begin_row, block_rows, end_row)
        rows_query = q_feat[begin_row:end_row]
        rows_grad = d_weighted[begin_row:end_row]
        scores = jnp.einsum(
            "if,jf->ij", rows_query, k_feat[:end_row], preferred_element_type=jnp.float32
        )
        scores_low = jnp.where(causal_mask, scores, 0.0).astype(jnp.bfloat16)
        grad_scores = (
            jnp.einsum("ie,je->ij", rows_grad, values[:end_row], preferred_element_type=jnp.float32)
            + d_totals[begin_row:end_row, None]
        )
        grad_scores = jnp.where(causal_mask, grad_scores, 0.0).astype(jnp.bfloat16)
        d_query.append(jnp.dot(grad_scores, k_feat[:end_row], preferred_element_type=jnp.float32))
        d_key = d_key.at[:end_row].add(
            jnp.einsum("ij,if->jf", grad_scores, rows_query, preferred_element_type=jnp.float32)
        )
        d_value = d_value.at[:end_row].add(
            jnp.einsum("ij,ie->je", scores_low, rows_grad, preferred_element_type=jnp.float32)
        )
    return (jnp.concatenate(d_query, 0), d_key, d_value)


def position_weights(length):
    angles = jnp.pi / 2.0 * jnp.arange(length, dtype=jnp.float32) / length
    return (jnp.cos(angles)[:, None], jnp.sin(angles)[:, None])


def fetch_params(
    query_key_value_weight,
    attention_out_weight,
    up_weight,
    down_weight,
    qk_bias,
    value_bias,
    out_bias,
    ffn_in_bias,
    ffn_out_bias,
    norm_gains,
    norm_biases,
):
    return (
        lax.all_gather(query_key_value_weight, "fsdp", axis=1, tiled=True),
        lax.all_gather(attention_out_weight, "fsdp", axis=1, tiled=True),
        lax.all_gather(up_weight, "fsdp", axis=0, tiled=True),
        lax.all_gather(down_weight, "fsdp", axis=1, tiled=True),
        lax.all_gather(qk_bias, "fsdp", axis=1, tiled=True),
        lax.all_gather(value_bias, "fsdp", axis=0, tiled=True),
        lax.all_gather(out_bias, "fsdp", axis=0, tiled=True),
        lax.all_gather(ffn_in_bias, "fsdp", axis=0, tiled=True),
        lax.all_gather(ffn_out_bias, "fsdp", axis=0, tiled=True),
        lax.all_gather(norm_gains, "fsdp", axis=1, tiled=True),
        lax.all_gather(norm_biases, "fsdp", axis=1, tiled=True),
    )


def run_forward(params, inputs):
    (
        query_key_value_weight,
        attention_out_weight,
        up_weight,
        down_weight,
        qk_bias,
        value_bias,
        out_bias,
        ffn_in_bias,
        ffn_out_bias,
        norm_gains,
        norm_biases,
    ) = params
    col_part = query_key_value_weight.shape[2]
    hidden_part = up_weight.shape[1]
    head_count = col_part // HEAD_DIM
    tp_place = lax.axis_index("tp")
    collected_rows = lax.all_gather(inputs, "tp", axis=1, tiled=True)
    seq_count, length = (collected_rows.shape[0], collected_rows.shape[1])
    proj_bias = jnp.concatenate(
        [
            lax.dynamic_slice_in_dim(qk_bias, tp_place * col_part, col_part, 1),
            lax.dynamic_slice_in_dim(value_bias[None, :], tp_place * col_part, col_part, 1),
        ],
        0,
    ).astype(jnp.float32)
    projected = (
        jnp.einsum(
            "ugn,anr->augr",
            collected_rows,
            query_key_value_weight,
            preferred_element_type=jnp.float32,
        )
        + proj_bias[:, None, None, :]
    )
    by_head = to_heads(projected, head_count)
    cosine, sine_w = position_weights(length)
    rect_query = jax.nn.relu(by_head[0])
    rect_key = jax.nn.relu(by_head[1])
    q_feat = jnp.concatenate([rect_query * cosine, rect_query * sine_w], -1).astype(jnp.bfloat16)
    k_feat = jnp.concatenate([rect_key * cosine, rect_key * sine_w], -1).astype(jnp.bfloat16)
    values = by_head[2].astype(jnp.bfloat16)
    weighted, totals = lax.map(attend, (q_feat, k_feat, values))
    context_rows = from_heads(weighted / jnp.maximum(totals, 1.0)[..., None], seq_count).astype(
        jnp.bfloat16
    )
    attention_partial_sum = jnp.einsum(
        "rtq,qj->rtj", context_rows, attention_out_weight, preferred_element_type=jnp.float32
    )
    attended = lax.psum_scatter(
        attention_partial_sum, "tp", scatter_dimension=1, tiled=True
    ) + out_bias.astype(jnp.float32)
    resid_one = inputs.astype(jnp.float32) + attended
    gains = norm_gains.astype(jnp.float32)
    shifts = norm_biases.astype(jnp.float32)
    normed_one = layer_norm(resid_one, gains[0], shifts[0])
    normalized_rows = lax.all_gather(normed_one.astype(jnp.bfloat16), "tp", axis=1, tiled=True)
    hidden_bias = lax.dynamic_slice_in_dim(ffn_in_bias, tp_place * hidden_part, hidden_part, 0)
    hidden_pre = jnp.einsum(
        "xwq,qp->xwp", normalized_rows, up_weight, preferred_element_type=jnp.float32
    ) + hidden_bias.astype(jnp.float32)
    hidden_activation = jax.nn.gelu(hidden_pre, approximate=False).astype(jnp.bfloat16)
    feedforward_partial_sum = jnp.einsum(
        "pem,mn->pen", hidden_activation, down_weight, preferred_element_type=jnp.float32
    )
    resid_two = (
        normed_one
        + lax.psum_scatter(feedforward_partial_sum, "tp", scatter_dimension=1, tiled=True)
        + ffn_out_bias.astype(jnp.float32)
    )
    result = layer_norm(resid_two, gains[1], shifts[1])
    return (
        result,
        collected_rows,
        by_head,
        q_feat,
        k_feat,
        values,
        weighted,
        totals,
        context_rows,
        resid_one,
        normed_one,
        normalized_rows,
        hidden_pre,
        hidden_activation,
        resid_two,
    )


def shards(
    inputs,
    query_key_value_weight,
    attention_out_weight,
    up_weight,
    down_weight,
    qk_bias,
    value_bias,
    out_bias,
    ffn_in_bias,
    ffn_out_bias,
    norm_gains,
    norm_biases,
    grad_out,
):
    fetched = fetch_params(
        query_key_value_weight,
        attention_out_weight,
        up_weight,
        down_weight,
        qk_bias,
        value_bias,
        out_bias,
        ffn_in_bias,
        ffn_out_bias,
        norm_gains,
        norm_biases,
    )
    output = run_forward(fetched, inputs)[0].astype(jnp.bfloat16)
    params_back = fetch_params(
        query_key_value_weight,
        attention_out_weight,
        up_weight,
        down_weight,
        qk_bias,
        value_bias,
        out_bias,
        ffn_in_bias,
        ffn_out_bias,
        norm_gains,
        norm_biases,
    )
    (
        result,
        collected_rows,
        by_head,
        q_feat,
        k_feat,
        values,
        weighted,
        totals,
        context_rows,
        resid_one,
        normed_one,
        normalized_rows,
        hidden_pre,
        hidden_activation,
        resid_two,
    ) = run_forward(params_back, inputs)
    (
        gathered_query_key_value,
        gathered_out_weight,
        gathered_up_weight,
        gathered_down_weight,
        full_qk_bias,
        full_value_bias,
        full_out_bias,
        full_ffn_in,
        full_ffn_out,
        full_gains,
        full_shifts,
    ) = params_back
    col_part = gathered_query_key_value.shape[2]
    hidden_part = gathered_up_weight.shape[1]
    model_width = inputs.shape[2]
    seq_count, length = (collected_rows.shape[0], collected_rows.shape[1])
    tp_place = lax.axis_index("tp")
    gains = full_gains.astype(jnp.float32)
    shifts = full_shifts.astype(jnp.float32)
    primal_two, second_back = jax.vjp(layer_norm, resid_two, gains[1], shifts[1])
    d_resid_two, d_gain_two, d_shift_two = second_back(grad_out.astype(jnp.float32))
    d_branch = d_resid_two.astype(jnp.bfloat16)
    d_ffn_out = jnp.sum(d_branch.astype(jnp.float32), (0, 1))
    branch_row_gradient = lax.all_gather(d_branch, "tp", axis=1, tiled=True)
    d_activated = jnp.einsum(
        "rcw,ew->rce", branch_row_gradient, gathered_down_weight, preferred_element_type=jnp.float32
    )
    grad_down = jnp.einsum(
        "job,joe->be", hidden_activation, branch_row_gradient, preferred_element_type=jnp.float32
    )
    primal_gelu, gelu_back = jax.vjp(partial(jax.nn.gelu, approximate=False), hidden_pre)
    hidden_gradient = gelu_back(d_activated)[0].astype(jnp.bfloat16)
    d_ffn_in = lax.dynamic_update_slice_in_dim(
        jnp.zeros((hidden_part * lax.axis_size("tp"),), jnp.float32),
        jnp.sum(hidden_gradient.astype(jnp.float32), (0, 1)),
        tp_place * hidden_part,
        0,
    )
    up_weight_gradient = jnp.einsum(
        "auf,aub->fb", normalized_rows, hidden_gradient, preferred_element_type=jnp.float32
    )
    normed_part_gradient = jnp.einsum(
        "oiu,ru->oir", hidden_gradient, gathered_up_weight, preferred_element_type=jnp.float32
    )
    d_normed = d_resid_two + lax.psum_scatter(
        normed_part_gradient, "tp", scatter_dimension=1, tiled=True
    )
    primal_one, first_back = jax.vjp(layer_norm, resid_one, gains[0], shifts[0])
    d_resid_one, d_gain_one, d_shift_one = first_back(d_normed)
    d_attended = d_resid_one.astype(jnp.bfloat16)
    d_out_bias = jnp.sum(d_attended.astype(jnp.float32), (0, 1))
    attention_row_gradient = lax.all_gather(d_attended, "tp", axis=1, tiled=True)
    d_context = to_heads(
        jnp.einsum(
            "prq,fq->prf",
            attention_row_gradient,
            gathered_out_weight,
            preferred_element_type=jnp.float32,
        ),
        col_part // HEAD_DIM,
    )
    grad_out_proj = jnp.einsum(
        "etz,etb->zb", context_rows, attention_row_gradient, preferred_element_type=jnp.float32
    )
    floor_den = jnp.maximum(totals, 1.0)
    d_weighted = (d_context / floor_den[..., None]).astype(jnp.bfloat16)
    d_totals = jnp.where(totals > 1.0, -jnp.sum(d_context * weighted, -1) / (totals * totals), 0.0)
    d_query, d_key, d_value = lax.map(attend_back, (q_feat, k_feat, values, d_weighted, d_totals))
    cosine, sine_w = position_weights(length)
    d_pre_query = (d_query[..., :HEAD_DIM] * cosine + d_query[..., HEAD_DIM:] * sine_w) * (
        by_head[0] > 0
    )
    d_pre_key = (d_key[..., :HEAD_DIM] * cosine + d_key[..., HEAD_DIM:] * sine_w) * (by_head[1] > 0)
    projected_gradient = from_heads(
        jnp.stack([d_pre_query, d_pre_key, d_value], 0), seq_count
    ).astype(jnp.bfloat16)
    d_proj_bias = jnp.sum(projected_gradient.astype(jnp.float32), (1, 2))
    d_qk_bias = lax.dynamic_update_slice_in_dim(
        jnp.zeros((2, model_width), jnp.float32), d_proj_bias[:2], tp_place * col_part, 1
    )
    d_value_bias = lax.dynamic_update_slice_in_dim(
        jnp.zeros((model_width,), jnp.float32), d_proj_bias[2], tp_place * col_part, 0
    )
    grad_qkv = jnp.einsum(
        "bkr,gbkn->grn", collected_rows, projected_gradient, preferred_element_type=jnp.float32
    )
    d_input_part = jnp.einsum(
        "chxr,cqr->hxq",
        projected_gradient,
        gathered_query_key_value,
        preferred_element_type=jnp.float32,
    )
    grad_input = d_resid_one + lax.psum_scatter(
        d_input_part.astype(jnp.bfloat16), "tp", scatter_dimension=1, tiled=True
    ).astype(jnp.float32)
    summed = (
        lax.psum_scatter(grad_qkv, "fsdp", scatter_dimension=1, tiled=True),
        lax.psum_scatter(grad_out_proj, "fsdp", scatter_dimension=1, tiled=True),
        lax.psum_scatter(up_weight_gradient, "fsdp", scatter_dimension=0, tiled=True),
        lax.psum_scatter(grad_down, "fsdp", scatter_dimension=1, tiled=True),
        lax.psum_scatter(d_qk_bias, "fsdp", scatter_dimension=1, tiled=True),
        lax.psum_scatter(d_value_bias, "fsdp", scatter_dimension=0, tiled=True),
        lax.psum_scatter(d_out_bias, "fsdp", scatter_dimension=0, tiled=True),
        lax.psum_scatter(d_ffn_in, "fsdp", scatter_dimension=0, tiled=True),
        lax.psum_scatter(d_ffn_out, "fsdp", scatter_dimension=0, tiled=True),
        lax.psum_scatter(
            jnp.stack([d_gain_one, d_gain_two], 0), "fsdp", scatter_dimension=1, tiled=True
        ),
        lax.psum_scatter(
            jnp.stack([d_shift_one, d_shift_two], 0), "fsdp", scatter_dimension=1, tiled=True
        ),
    )
    smalls = lax.psum(
        (summed[4], summed[5], summed[6], summed[7], summed[8], summed[9], summed[10]), "tp"
    )
    return (
        output,
        grad_input,
        summed[0],
        summed[1],
        summed[2],
        summed[3],
        smalls[0],
        smalls[1],
        smalls[2],
        smalls[3],
        smalls[4],
        smalls[5],
        smalls[6],
    )


def solution(mesh):
    return jax.shard_map(
        shards,
        mesh=mesh,
        in_specs=(
            P("fsdp", "tp", None),
            P(None, "fsdp", "tp"),
            P("tp", "fsdp"),
            P("fsdp", "tp"),
            P("tp", "fsdp"),
            P(None, "fsdp"),
            P("fsdp"),
            P("fsdp"),
            P("fsdp"),
            P("fsdp"),
            P(None, "fsdp"),
            P(None, "fsdp"),
            P("fsdp", "tp", None),
        ),
        out_specs=(
            P("fsdp", "tp", None),
            P("fsdp", "tp", None),
            P(None, "fsdp", "tp"),
            P("tp", "fsdp"),
            P("fsdp", "tp"),
            P("tp", "fsdp"),
            P(None, "fsdp"),
            P("fsdp"),
            P("fsdp"),
            P("fsdp"),
            P("fsdp"),
            P(None, "fsdp"),
            P(None, "fsdp"),
        ),
        check_vma=False,
    )
```

profile of v0, /device:TPU:0, one launch (start us, length us, event | category | flops | bytes accessed | tf_op | source)
XLA Modules:
  0.0 1445.1 jit_solution(8393627865911952048)
XLA Ops:
  14.8 78.8 %all-reduce.13 = (bf16[768]{0:T(1024)(128)(2,1)S(1)}, bf16[768]{0:T(1024)(128)(2,1)S(1)}, bf16[3072]{0:T(1024)(128)(2,1)S(1)}, bf16[768]{0:T(1024)(128)(2,1)S(1)}) all-reduce(bf16[768]{0:T(1024)(128)(2,1)S(1)} %dynamic-update-slice.12, bf16[768]{0:T(1024)(128)(2,1)S(1)} %dynamic-update-slice.13, ...), channel_id=1, replica_groups=mesh['fsdp'=16,'tp'=2] {'fsdp'}, use_global_device_ids=true, to_apply=%add.2 | all-reduce | flops 5376 | bytes 21504
  93.6 35.5 %all-gather = bf16[16,48,2]{1,2,0:T(2,128)(2,1)S(1)} all-gather(bf16[1,48,2]{1,2,0:T(2,128)(2,1)} %bitcast.346), channel_id=1, replica_groups=mesh['fsdp'=16,'tp'=2] {'fsdp'}, dimensions={0}, use_global_device_ids=true | all-gather | bytes 3264 | tf_op jit(solution)/shard_map/all_gather | solution.py:121
  129.3 43.2 %all_gather.62 = bf16[384,768]{0,1:T(8,128)(2,1)} all-gather(bf16[384,48]{0,1:T(8,128)(2,1)} %param.31), channel_id=1, replica_groups=mesh['fsdp'=16,'tp'=2] {'fsdp'}, dimensions={1}, use_global_device_ids=true | all-gather | bytes 626688 | tf_op jit(solution)/shard_map/all_gather | solution.py:118
  172.5 4.3 bitcast_add_fusion
  184.1 25.9 %while.42 = (s32[]{:T(128)}, f32[6,1024,64]{1,2,0:T(8,128)}, f32[6,1024]{1,0:T(8,128)S(1)}, bf16[6,1024,128]{2,1,0:T(8,128)(2,1)}, bf16[6,1024,128]{2,1,0:T(8,128)(2,1)S(1)}, /*index=5*/bf16[6,1024,64]{2,1,0:T(8,128)(2,1)S(1)}) while((s32[]{:T(128)}, f32[6,1024,64]{1,2,0:T(8,128)}, f32[6,1024]{1,0:T(8,128)S(1)}, ...), condition=%wide.region_3.4_spmd.clone, body=%wide.region_0.3_spmd.sunk.clone | while | flops 306250240 | bytes 5010017 | solution.py:174
  217.0 35.3 %all-gather.1 = bf16[16,48,2]{1,2,0:T(2,128)(2,1)S(1)} all-gather(bf16[1,48,2]{1,2,0:T(2,128)(2,1)S(1)} %bitcast.347), channel_id=1, replica_groups=mesh['fsdp'=16,'tp'=2] {'fsdp'}, dimensions={0}, use_global_device_ids=true | all-gather | bytes 3264 | tf_op jit(solution)/shard_map/all_gather | solution.py:126
  252.4 37.4 %all-gather.2 = bf16[16,48,2]{1,2,0:T(2,128)(2,1)S(1)} all-gather(bf16[1,48,2]{1,2,0:T(2,128)(2,1)S(1)} %bitcast.348), channel_id=1, replica_groups=mesh['fsdp'=16,'tp'=2] {'fsdp'}, dimensions={0}, use_global_device_ids=true | all-gather | bytes 3264 | tf_op jit(solution)/shard_map/all_gather | solution.py:127
  294.5 6.1 all-gather.15.cloned.1.call-done
  300.6 19.9 %multiply_convert_fusion = (bf16[1024,1536]{1,0:T(8,128)(2,1)}, f32[1024,1536]{1,0:T(8,128)}, f32[1024,1536]{1,0:T(8,128)}) fusion(f32[1536]{0:T(1024)S(1)} %dynamic-slice_convert_fusion, bf16[768,1536]{1,0:T(8,128)(2,1)} %all-gather.17.cloned.1.call-done, bf16[1,1024,768]{2,1,0:T(8,128)(2,1)} %all-gather.15.cloned.1.call-done), kind=kOutput, calls=%fused_computation.82 | convolution fusion | flops 2519728128 | bytes 19666944 | tf_op jit(solution)/shard_map/xwq,qp->xwp/dot_general | solution.py:190
  320.4 46.7 %all-gather.19.cloned.1.call-done = bf16[1536,768]{0,1:T(8,128)(2,1)} async-done(((bf16[1536,48]{0,1:T(8,128)(2,1)}), bf16[1536,768]{0,1:T(8,128)(2,1)}) %all-gather.19.cloned.1.call-update) | async-done | bytes 2359312 | tf_op jit(solution)/shard_map/all_gather | solution.py:120
  367.1 6.9 convolution_bitcast_fusion.2
  374.1 9.8 reduce-scatter.19.cloned.1.call-done
  391.3 10.9 all-gather.21.cloned.1.call-done
  402.2 10.9 convert_reduce_fusion
  414.8 4.3 convolution_bitcast_fusion.1
  419.2 12.2 reduce-scatter.21.cloned.1.call-done
  440.7 7.5 all-gather.23.cloned.1.call-done
  451.3 76.9 %while.43 = (s32[]{:T(128)}, f32[6,1024,128]{1,2,0:T(8,128)}, f32[6,1024,128]{1,2,0:T(8,128)}, bf16[6,1024,64]{1,2,0:T(8,128)(2,1)S(1)}, bf16[6,1024,64]{1,2,0:T...) while((s32[]{:T(128)}, f32[6,1024,128]{1,2,0:T(8,128)}, ...), condition=%wide.region_17.18_spmd.clone, body=%wide.region_16.17_spmd.sunk.clone | while | flops 811139584 | bytes 14052473 | solution.py:349
  528.3 5.0 select_bitcast_fusion.1
  535.1 4.9 fusion.87
  540.0 4.1 convolution_bitcast_fusion
  549.6 6.3 fusion.71
  557.7 5.8 fusion.77
  569.9 6.5 reduce-scatter.35.cloned.1.call-done
  577.2 124.4 %reduce-scatter.33.cloned.1.call-done = f32[48,2]{1,0:T(8,128)} async-done(((f32[768,2]{1,0:T(8,128)}), f32[48,2]{1,0:T(8,128)}) %reduce-scatter.33.cloned.1.call-update) | async-done | bytes 400
  702.7 74.9 %all-reduce.11 = (f32[768]{0:T(1024)S(1)}, f32[768]{0:T(1024)S(1)}, f32[3072]{0:T(1024)S(1)}, f32[768]{0:T(1024)S(1)}) all-reduce(f32[768]{0:T(1024)S(1)} %dynamic_update_slice.42, f32[768]{0:T(1024)S(1)} %copy-done.17, f32[3072]{0:T(1024)S(1)} %dynamic_update_slice.43, ...), channel_id=11, replica_groups=mesh['fsdp'=16,'tp'=2] {'fsdp'}, use_global_device_ids=true, to_apply=%region_26.27.clone | all-reduce | flops 5376 | bytes 43008
  777.9 49.8 %reduce-scatter.31.cloned.1.call-done = f32[48,2]{1,0:T(8,128)} async-done(((f32[768,2]{1,0:T(8,128)}), f32[48,2]{1,0:T(8,128)}) %reduce-scatter.31.cloned.1.call-update) | async-done | bytes 400
  831.5 7.0 reduce-scatter.23.cloned.1.call-done
  841.1 184.9 %all-reduce.16.cloned.1.call-done = f32[3,768,384]{2,0,1:T(4,128)} async-done(((f32[3,768,384]{2,0,1:T(4,128)}), f32[3,768,384]{2,0,1:T(4,128)}) %all-reduce.16.cloned.1.call-update) | async-done | bytes 3538960
  1027.7 139.6 %reduce-scatter.29.cloned.1.call-done = f32[1536,48]{0,1:T(8,128)} async-done(((f32[1536,768]{0,1:T(8,128)}), f32[1536,48]{0,1:T(8,128)}) %reduce-scatter.29.cloned.1.call-update) | async-done | bytes 294928 | tf_op jit(solution)/shard_map/reduce_scatter | solution.py:381
  1167.4 142.7 %reduce-scatter.27.cloned.1.call-done = f32[48,1536]{1,0:T(8,128)} async-done(((f32[768,1536]{1,0:T(8,128)}), f32[48,1536]{1,0:T(8,128)}) %reduce-scatter.27.cloned.1.call-update) | async-done | bytes 294928 | tf_op jit(solution)/shard_map/reduce_scatter | solution.py:380
  1310.1 127.8 %reduce-scatter.25.cloned.1.call-done = f32[384,48]{0,1:T(8,128)} async-done(((f32[384,768]{0,1:T(8,128)}), f32[384,48]{0,1:T(8,128)}) %reduce-scatter.25.cloned.1.call-update) | async-done | bytes 73744 | tf_op jit(solution)/shard_map/reduce_scatter | solution.py:379
  (313 shorter events, 173.1 us)
Async XLA Ops:
  7.2 165.4 %all-gather.13.cloned.1.call-start = ((), (), s32[]{:S(2)}) async-start(), calls=%async_computation.11 | async-start | bytes 2359296 | tf_op jit(solution)/shard_map/all_gather | solution.py:149
  7.9 164.6 %all-gather.11.cloned.1.call-start = ((), (), s32[]{:S(2)}) async-start(), calls=%async_computation.10 | async-start | bytes 1880064 | tf_op jit(solution)/shard_map/all_gather | solution.py:117
  8.7 281.3 %reduce-scatter.17.cloned.1.call-start = ((), (), s32[]{:S(2)}) async-start(), calls=%async_computation.12 | async-start | bytes 4718592 | tf_op jit(solution)/shard_map/reduce_scatter | solution.py:181
  176.9 2.3 copy-start.2
  210.0 6.4 copy-start.3
  210.0 6.4 copy-start.6
  210.0 3.7 copy-start.4
  216.3 36.1 %copy-start.20 = (bf16[2,48]{1,0:T(2,128)(2,1)S(1)}, bf16[2,48]{1,0:T(2,128)(2,1)}, u32[]{:S(2)}) copy-start(bf16[2,48]{1,0:T(2,128)(2,1)} %param.40) | copy-start | bytes 580
  216.3 73.6 %copy-start.8 = (bf16[1,512,768]{2,1,0:T(8,128)(2,1)S(1)}, bf16[1,512,768]{2,1,0:T(8,128)(2,1)}, u32[]{:S(2)}) copy-start(bf16[1,512,768]{2,1,0:T(8,128)(2,1)} %param.29) | copy-start | bytes 2359300
  216.4 78.1 %all-gather.17.cloned.1.call-start = ((), (), s32[]{:S(2)}) async-start(), calls=%async_computation.14 | async-start | bytes 2506752 | tf_op jit(solution)/shard_map/all_gather | solution.py:119
  217.0 83.6 %all-gather.15.cloned.1.call-start = ((), (), s32[]{:S(2)}) async-start(), calls=%async_computation.13 | async-start | bytes 2359296 | tf_op jit(solution)/shard_map/all_gather | solution.py:188
  293.2 73.9 %all-gather.19.cloned.1.call-start = ((), (), s32[]{:S(2)}) async-start(), calls=%async_computation.15 | async-start | bytes 2506752 | tf_op jit(solution)/shard_map/all_gather | solution.py:120
  293.8 90.1 %reduce-scatter.19.cloned.1.call-start = ((), (), s32[]{:S(2)}) async-start(), calls=%async_computation.16 | async-start | bytes 4718592 | tf_op jit(solution)/shard_map/reduce_scatter | solution.py:199
  374.1 28.1 %all-gather.21.cloned.1.call-start = ((), (), s32[]{:S(2)}) async-start(), calls=%async_computation.17 | async-start | bytes 2359296 | tf_op jit(solution)/shard_map/all_gather | solution.py:305
  391.1 40.3 %reduce-scatter.21.cloned.1.call-start = ((), (), s32[]{:S(2)}) async-start(), calls=%async_computation.18 | async-start | bytes 4718592 | tf_op jit(solution)/shard_map/reduce_scatter | solution.py:326
  402.2 12.6 copy-start.21
  419.1 29.1 %all-gather.23.cloned.1.call-start = ((), (), s32[]{:S(2)}) async-start(), calls=%async_computation.19 | async-start | bytes 2359296 | tf_op jit(solution)/shard_map/all_gather | solution.py:333
  437.1 11.1 copy-start.14
  437.1 139.3 %reduce-scatter.35.cloned.1.call-start = ((), (), s32[]{:S(2)}) async-start(), calls=%async_computation.26 | async-start | bytes 417792
  438.2 10.0 copy-start.15
  439.3 262.3 %reduce-scatter.33.cloned.1.call-start = ((), (), s32[]{:S(2)}) async-start(), calls=%async_computation.25 | async-start | bytes 417792
  440.4 387.3 %reduce-scatter.31.cloned.1.call-start = ((), (), s32[]{:S(2)}) async-start(), calls=%async_computation.24 | async-start | bytes 417792
  533.7 6.3 copy-start.13
  535.0 303.6 %reduce-scatter.23.cloned.1.call-start = ((), (), s32[]{:S(2)}) async-start(), calls=%async_computation.20 | async-start | bytes 2359296 | tf_op jit(solution)/shard_map/reduce_scatter | solution.py:374
  540.0 486.1 %all-reduce.16.cloned.1.call-start = ((), (), s32[]{:S(2)}) async-start(), calls=%async_computation.27 | async-start | bytes 9437184
  548.2 619.2 %reduce-scatter.29.cloned.1.call-start = ((), (), s32[]{:S(2)}) async-start(), calls=%async_computation.23 | async-start | bytes 5013504 | tf_op jit(solution)/shard_map/reduce_scatter | solution.py:381
  555.9 754.2 %reduce-scatter.27.cloned.1.call-start = ((), (), s32[]{:S(2)}) async-start(), calls=%async_computation.22 | async-start | bytes 5013504 | tf_op jit(solution)/shard_map/reduce_scatter | solution.py:380
  563.5 6.0 copy-start.18
  563.6 139.1 %copy-start.16 = (f32[768]{0:T(1024)S(1)}, f32[768]{0:T(1024)}, u32[]{:S(2)}) copy-start(f32[768]{0:T(1024)} %get-tuple-element.445) | copy-start | bytes 9220
  563.6 139.1 %copy-start.17 = (f32[768]{0:T(1024)S(1)}, f32[768]{0:T(1024)}, u32[]{:S(2)}) copy-start(f32[768]{0:T(1024)} %get-tuple-element.447) | copy-start | bytes 9220
  563.6 874.4 %reduce-scatter.25.cloned.1.call-start = ((), (), s32[]{:S(2)}) async-start(), calls=%async_computation.21 | async-start | bytes 1253376 | tf_op jit(solution)/shard_map/reduce_scatter | solution.py:379
  564.7 273.9 %copy-start.1 = (f32[1,512,768]{2,1,0:T(8,128)S(1)}, f32[1,512,768]{2,1,0:T(8,128)}, u32[]{:S(2)}) copy-start(f32[1,512,768]{2,1,0:T(8,128)} %copy-done) | copy-start | bytes 4718596
  (9 other events, 11.7 us)
Sparse Core Ops, SparseCore 0:
  9.6 12.4 all-gather.12
  24.8 60.3 all-gather.10
  216.5 6.7 reduce-scatter.16
  226.3 63.4 all-gather.16
  293.3 7.1 all-gather.14
  303.6 63.4 all-gather.18
  374.2 9.7 reduce-scatter.18
  391.2 10.9 all-gather.20
  419.2 12.0 reduce-scatter.20
  437.2 10.9 all-gather.22
  453.6 122.7 reduce-scatter.34
  580.9 120.6 reduce-scatter.32
  707.0 120.6 reduce-scatter.30
  830.4 8.1 reduce-scatter.22
  845.1 180.8 all-reduce.15
  1031.6 135.7 reduce-scatter.28
  1173.8 136.2 reduce-scatter.26
  1315.3 122.6 reduce-scatter.24
where the time goes:
time: 1450 us
  waiting for transfers between devices  879 us (61%)
  blocking collectives  308 us (21%)
  matrix products  164 us (11%)
  local copies, waits for them, and re-layouts  42.6 us (3%)
  other arithmetic  31 us (2%)
  between operations  17.7 us (1%)
    unnamed x22, waiting for transfers between devices  368 us
    unnamed x2, blocking collectives  154 us
    reduce_scatter x1, waiting for transfers between devices, shards(): lax.psum_scatter(up_weight_gradient, 'fsdp', scatter_dimension=0, tiled=T...  143 us
    reduce_scatter x1, waiting for transfers between devices, shards(): lax.psum_scatter(grad_down, 'fsdp', scatter_dimension=1, tiled=True)  140 us
    reduce_scatter x1, waiting for transfers between devices, shards(): lax.psum_scatter(grad_out_proj, 'fsdp', scatter_dimension=1, tiled=True)  128 us
    all_gather x1, waiting for transfers between devices, fetch_params(): lax.all_gather(down_weight, 'fsdp', axis=1, tiled=True)  46.7 us
    all_gather x1, blocking collectives, fetch_params(): lax.all_gather(attention_out_weight, 'fsdp', axis=1, tiled=True)  43.2 us
    all_gather x1, blocking collectives, fetch_params(): lax.all_gather(norm_biases, 'fsdp', axis=1, tiled=True)  37.4 us
  transfers between devices with their start and end apart: 18, of which 14 were waited for; matrix products, arithmetic and copies ran while one was open for 11% of the time, Pallas kernels for 0%

commit v1 on v0

--- a/solution.py
+++ b/solution.py
@@ -3,9 +3,270 @@
 import jax
 import jax.numpy as jnp
 from jax import lax
+from jax.experimental import pallas as pl
+from jax.experimental.pallas import tpu as pltpu
 from jax.sharding import PartitionSpec as P
 
 HEAD_DIM = 64
+MESH = pl.DeviceIdType.MESH
+BF16 = jnp.bfloat16
+F32 = jnp.float32
+
+GRID = (4, 2, 2)
+
+
+def place():
+    f = lax.axis_index("fsdp")
+    return lax.rem(f, 2), lax.rem(f // 2, 2), f // 4, lax.axis_index("tp")
+
+
+def rank(x, y, z):
+    return (z * 2 + y) * 2 + x
+
+
+def peers(x, y, z, t):
+    return (
+        [(rank(x, y, lax.rem(z + k, 4)), t) for k in (1, 2, 3)],
+        (rank(1 - x, y, z), t),
+        (rank(x, 1 - y, z), t),
+        (rank(x, y, z), 1 - t),
+    )
+
+
+def meet(devices):
+    barrier = pltpu.get_barrier_semaphore()
+    for device in devices:
+        pl.semaphore_signal(barrier, inc=1, device_id=device, device_id_type=MESH)
+    pl.semaphore_wait(barrier, len(devices))
+
+
+def remote(source, target, send_sem, recv_sem, device):
+    return pltpu.make_async_remote_copy(
+        src_ref=source,
+        dst_ref=target,
+        send_sem=send_sem,
+        recv_sem=recv_sem,
+        device_id=device,
+        device_id_type=MESH,
+    )
+
+
+def gather_kernel(chunks, ahead, w_ref, whole, send, recv, own):
+    x, y, z, t = place()
+    z_peers, x_peer, y_peer, _ = peers(x, y, z, t)
+    meet(z_peers + [x_peer, y_peer])
+    local = pltpu.make_async_copy(w_ref, whole.at[:, z, y, x], own)
+    local.start()
+    sends = []
+
+    def go(source, chunk, stage, device):
+        copy = remote(source, source, send.at[chunk, stage], recv.at[chunk, stage], device)
+        copy.start()
+        sends.append(copy)
+
+    def arrive(target, chunk, stage):
+        remote(target, target, send.at[chunk, stage], recv.at[chunk, stage], x_peer).wait_recv()
+
+    def along_z(chunk):
+        for k in range(3):
+            copy = remote(
+                w_ref.at[chunk],
+                whole.at[chunk, z, y, x],
+                send.at[chunk, k],
+                recv.at[chunk, k],
+                z_peers[k],
+            )
+            copy.start()
+            sends.append(copy)
+
+    def second(chunk):
+        for k in range(3):
+            arrive(whole.at[chunk, lax.rem(z + 3 - k, 4), y, x], chunk, k)
+        go(whole.at[chunk, :, y, x], chunk, 3, x_peer if chunk % 2 else y_peer)
+
+    def third(chunk):
+        if chunk % 2:
+            arrive(whole.at[chunk, :, y, 1 - x], chunk, 3)
+            go(whole.at[chunk, :, y], chunk, 4, y_peer)
+        else:
+            arrive(whole.at[chunk, :, 1 - y, x], chunk, 3)
+            go(whole.at[chunk, :, :, x], chunk, 4, x_peer)
+
+    for chunk in range(min(ahead, chunks)):
+        along_z(chunk)
+    local.wait()
+    for step in range(chunks + 1):
+        if step < chunks:
+            second(step)
+        if step + ahead < chunks:
+            along_z(step + ahead)
+        if step >= 1:
+            third(step - 1)
+    for chunk in range(chunks):
+        arrive(whole.at[chunk, :, 1 - y] if chunk % 2 else whole.at[chunk, :, :, 1 - x], chunk, 4)
+    for copy in sends:
+        copy.wait_send()
+
+
+def scatter_kernel(chunks, g_ref, s_ref, o_ref, os_ref, r1, r2, r3, q1, q2, q3, q4, send, recv, ssend, srecv):
+    x, y, z, t = place()
+    z_peers, x_peer, y_peer, partner = peers(x, y, z, t)
+    meet(z_peers + [x_peer, y_peer, partner])
+    sends = []
+
+    def go(source, target, s, r, device):
+        copy = remote(source, target, s, r, device)
+        copy.start()
+        sends.append(copy)
+
+    def arrive(target, s, r):
+        remote(target, target, s, r, x_peer).wait_recv()
+
+    def first(chunk):
+        go(
+            g_ref.at[chunk, :, 1 - y] if chunk % 2 else g_ref.at[chunk, :, :, 1 - x],
+            r1.at[chunk],
+            send.at[chunk, 0],
+            recv.at[chunk, 0],
+            y_peer if chunk % 2 else x_peer,
+        )
+
+    def second(chunk):
+        arrive(r1.at[chunk], send.at[chunk, 0], recv.at[chunk, 0])
+        for q in range(4):
+            for r in range(2):
+                mine = g_ref[chunk, q, y, r] if chunk % 2 else g_ref[chunk, q, r, x]
+                r1[chunk, q, r] = (mine.astype(F32) + r1[chunk, q, r].astype(F32)).astype(BF16)
+        go(
+            r1.at[chunk, :, 1 - x] if chunk % 2 else r1.at[chunk, :, 1 - y],
+            r2.at[chunk],
+            send.at[chunk, 1],
+            recv.at[chunk, 1],
+            x_peer if chunk % 2 else y_peer,
+        )
+
+    def third(chunk):
+        arrive(r2.at[chunk], send.at[chunk, 1], recv.at[chunk, 1])
+        for q in range(4):
+            mine = r1[chunk, q, x] if chunk % 2 else r1[chunk, q, y]
+            r2[chunk, q] = (mine.astype(F32) + r2[chunk, q].astype(F32)).astype(BF16)
+        for k in range(3):
+            go(
+                r2.at[chunk, lax.rem(z + k + 1, 4)],
+                r3.at[chunk, k],
+                send.at[chunk, 2 + k],
+                recv.at[chunk, 2 + k],
+                z_peers[k],
+            )
+
+    def last(chunk):
+        total = r2[chunk, z].astype(F32)
+        for k in range(3):
+            arrive(r3.at[chunk, k], send.at[chunk, 2 + k], recv.at[chunk, 2 + k])
+            total = total + r3[chunk, k].astype(F32)
+        o_ref[chunk] = total
+
+    go(s_ref.at[:, :, 1 - x], q1, ssend.at[0], srecv.at[0], x_peer)
+    for chunk in range(chunks):
+        first(chunk)
+    arrive(q1, ssend.at[0], srecv.at[0])
+    q1[...] = q1[...] + s_ref[:, :, x]
+    go(q1.at[:, 1 - y], q2, ssend.at[1], srecv.at[1], y_peer)
+    for step in range(chunks + 4):
+        if step < chunks:
+            second(step)
+        if step == 1:
+            arrive(q2, ssend.at[1], srecv.at[1])
+            q2[...] = q2[...] + q1[:, y]
+            for k in range(3):
+                go(q2.at[lax.rem(z + k + 1, 4)], q3.at[k], ssend.at[2 + k], srecv.at[2 + k], z_peers[k])
+        if step == 3:
+            total = q2[z]
+            for k in range(3):
+                arrive(q3.at[k], ssend.at[2 + k], srecv.at[2 + k])
+                total = total + q3[k]
+            q4[0] = total
+            go(q4.at[0], q4.at[1], ssend.at[5], srecv.at[5], partner)
+        if 0 <= step - 2 < chunks:
+            third(step - 2)
+        if 0 <= step - 4 < chunks:
+            last(step - 4)
+    arrive(q4.at[1], ssend.at[5], srecv.at[5])
+    os_ref[...] = q4[0] + q4[1]
+    for copy in sends:
+        copy.wait_send()
+
+
+VMEM = pl.BlockSpec(memory_space=pltpu.VMEM)
+DMA = pltpu.SemaphoreType.DMA
+
+
+def gather_rows(stack):
+    chunks, rows, cols = stack.shape
+    ranks = lax.axis_size("fsdp")
+    if ranks != 16 or rows % 16:
+        return lax.all_gather(stack, "fsdp", axis=1, tiled=True)
+    whole = pl.pallas_call(
+        partial(gather_kernel, chunks, 3),
+        name="gather_rows",
+        out_shape=jax.ShapeDtypeStruct((chunks,) + GRID + (rows, cols), stack.dtype),
+        in_specs=[VMEM],
+        out_specs=VMEM,
+        scratch_shapes=[DMA((chunks, 5)), DMA((chunks, 5)), DMA],
+        compiler_params=pltpu.CompilerParams(
+            collective_id=0, has_side_effects=True, vmem_limit_bytes=40 << 20
+        ),
+    )(stack)
+    return whole.reshape(chunks, ranks * rows, cols)
+
+
+def scatter_rows(stack, small):
+    chunks, rows, cols = stack.shape
+    ranks = lax.axis_size("fsdp")
+    rows //= ranks
+    if ranks != 16 or rows % 16:
+        return (
+            lax.psum_scatter(stack, "fsdp", scatter_dimension=1, tiled=True),
+            lax.psum(lax.psum_scatter(small, "fsdp", scatter_dimension=0, tiled=True), "tp")[0],
+        )
+    stack = stack.astype(BF16).reshape((chunks,) + GRID + (rows, cols))
+    small = small.reshape(GRID + small.shape[1:])
+    tail = small.shape[3:]
+    return pl.pallas_call(
+        partial(scatter_kernel, chunks),
+        name="scatter_rows",
+        out_shape=(
+            jax.ShapeDtypeStruct((chunks, rows, cols), F32),
+            jax.ShapeDtypeStruct(tail, F32),
+        ),
+        in_specs=[VMEM, VMEM],
+        out_specs=(VMEM, VMEM),
+        scratch_shapes=[
+            pltpu.VMEM((chunks, 4, 2, rows, cols), BF16),
+            pltpu.VMEM((chunks, 4, rows, cols), BF16),
+            pltpu.VMEM((chunks, 3, rows, cols), BF16),
+            pltpu.VMEM((4, 2) + tail, F32),
+            pltpu.VMEM((4,) + tail, F32),
+            pltpu.VMEM((3,) + tail, F32),
+            pltpu.VMEM((2,) + tail, F32),
+            DMA((chunks, 5)),
+            DMA((chunks, 5)),
+            DMA((6,)),
+            DMA((6,)),
+        ],
+        compiler_params=pltpu.CompilerParams(
+            collective_id=1, has_side_effects=True, vmem_limit_bytes=48 << 20
+        ),
+    )(stack, small)
+
+
+def split_cols(matrix, cols):
+    rows = matrix.shape[0]
+    return jnp.moveaxis(matrix.reshape(rows, -1, cols), 1, 0)
+
+
+def join_cols(chunks):
+    return jnp.moveaxis(chunks, 0, 1).reshape(chunks.shape[1], -1)
 
 
 norm_eps = 1e-05
@@ -113,18 +374,46 @@
     norm_gains,
     norm_biases,
 ):
+    col_part = query_key_value_weight.shape[2]
+    hidden_chunks = up_weight.shape[1] // col_part
+    rows = query_key_value_weight.shape[1]
+    small = jnp.concatenate(
+        [
+            v.reshape(-1, rows)
+            for v in (qk_bias, value_bias, out_bias, ffn_in_bias, ffn_out_bias, norm_gains, norm_biases)
+        ],
+        0,
+    )
+    small = jnp.pad(small.T, ((0, 0), (0, col_part - small.shape[0])))
+    stack = jnp.concatenate(
+        [
+            small[None],
+            query_key_value_weight,
+            attention_out_weight.T[None],
+            split_cols(up_weight, col_part),
+            split_cols(down_weight.T, col_part),
+        ],
+        0,
+    )
+    whole = gather_rows(stack)
+    small = whole[0].T
+    hidden = ffn_in_bias.shape[0] // rows
+    ranks = lax.axis_size("fsdp")
+    in_bias = small[4 : 4 + hidden].reshape(hidden, ranks, rows)
+    in_bias = jnp.moveaxis(in_bias, 1, 0).reshape(-1)
+    after = 4 + hidden
     return (
-        lax.all_gather(query_key_value_weight, "fsdp", axis=1, tiled=True),
-        lax.all_gather(attention_out_weight, "fsdp", axis=1, tiled=True),
-        lax.all_gather(up_weight, "fsdp", axis=0, tiled=True),
-        lax.all_gather(down_weight, "fsdp", axis=1, tiled=True),
-        lax.all_gather(qk_bias, "fsdp", axis=1, tiled=True),
-        lax.all_gather(value_bias, "fsdp", axis=0, tiled=True),
-        lax.all_gather(out_bias, "fsdp", axis=0, tiled=True),
-        lax.all_gather(ffn_in_bias, "fsdp", axis=0, tiled=True),
-        lax.all_gather(ffn_out_bias, "fsdp", axis=0, tiled=True),
-        lax.all_gather(norm_gains, "fsdp", axis=1, tiled=True),
-        lax.all_gather(norm_biases, "fsdp", axis=1, tiled=True),
+        whole[1:4],
+        whole[4].T,
+        join_cols(whole[5 : 5 + hidden_chunks]),
+        join_cols(whole[5 + hidden_chunks :]).T,
+        small[0:2],
+        small[2],
+        small[3],
+        in_bias,
+        small[after],
+        small[after + 1 : after + 3],
+        small[after + 3 : after + 5],
     )
 
 
@@ -234,20 +523,6 @@
     norm_biases,
     grad_out,
 ):
-    fetched = fetch_params(
-        query_key_value_weight,
-        attention_out_weight,
-        up_weight,
-        down_weight,
-        qk_bias,
-        value_bias,
-        out_bias,
-        ffn_in_bias,
-        ffn_out_bias,
-        norm_gains,
-        norm_biases,
-    )
-    output = run_forward(fetched, inputs)[0].astype(jnp.bfloat16)
     params_back = fetch_params(
         query_key_value_weight,
         attention_out_weight,
@@ -278,6 +553,7 @@
         hidden_activation,
         resid_two,
     ) = run_forward(params_back, inputs)
+    output = result.astype(jnp.bfloat16)
     (
         gathered_query_key_value,
         gathered_out_weight,
@@ -374,40 +650,53 @@
     grad_input = d_resid_one + lax.psum_scatter(
         d_input_part.astype(jnp.bfloat16), "tp", scatter_dimension=1, tiled=True
     ).astype(jnp.float32)
-    summed = (
-        lax.psum_scatter(grad_qkv, "fsdp", scatter_dimension=1, tiled=True),
-        lax.psum_scatter(grad_out_proj, "fsdp", scatter_dimension=1, tiled=True),
-        lax.psum_scatter(up_weight_gradient, "fsdp", scatter_dimension=0, tiled=True),
-        lax.psum_scatter(grad_down, "fsdp", scatter_dimension=1, tiled=True),
-        lax.psum_scatter(d_qk_bias, "fsdp", scatter_dimension=1, tiled=True),
-        lax.psum_scatter(d_value_bias, "fsdp", scatter_dimension=0, tiled=True),
-        lax.psum_scatter(d_out_bias, "fsdp", scatter_dimension=0, tiled=True),
-        lax.psum_scatter(d_ffn_in, "fsdp", scatter_dimension=0, tiled=True),
-        lax.psum_scatter(d_ffn_out, "fsdp", scatter_dimension=0, tiled=True),
-        lax.psum_scatter(
-            jnp.stack([d_gain_one, d_gain_two], 0), "fsdp", scatter_dimension=1, tiled=True
-        ),
-        lax.psum_scatter(
-            jnp.stack([d_shift_one, d_shift_two], 0), "fsdp", scatter_dimension=1, tiled=True
-        ),
-    )
-    smalls = lax.psum(
-        (summed[4], summed[5], summed[6], summed[7], summed[8], summed[9], summed[10]), "tp"
-    )
+    ranks = lax.axis_size("fsdp")
+    rows = model_width // ranks
+    small = jnp.concatenate(
+        [
+            jnp.moveaxis(v.reshape(-1, ranks, rows), 1, 0)
+            for v in (
+                d_qk_bias,
+                d_value_bias,
+                d_out_bias,
+                d_ffn_out,
+                d_gain_one,
+                d_gain_two,
+                d_shift_one,
+                d_shift_two,
+            )
+        ]
+        + [d_ffn_in.reshape(ranks, -1, rows)],
+        1,
+    )
+    kinds = small.shape[1]
+    small = jnp.pad(small.reshape(ranks, -1), ((0, 0), (0, 1024 - kinds * rows)))
+    stack = jnp.concatenate(
+        [
+            grad_qkv,
+            grad_out_proj.T[None],
+            split_cols(up_weight_gradient, col_part),
+            split_cols(grad_down.T, col_part),
+        ],
+        0,
+    )
+    owned, small = scatter_rows(stack, small.reshape(ranks, 8, 128))
+    small = small.reshape(-1)[: kinds * rows].reshape(kinds, rows)
+    hidden_chunks = hidden_part // col_part
     return (
         output,
         grad_input,
-        summed[0],
-        summed[1],
-        summed[2],
-        summed[3],
-        smalls[0],
-        smalls[1],
-        smalls[2],
-        smalls[3],
-        smalls[4],
-        smalls[5],
-        smalls[6],
+        owned[:3],
+        owned[3].T,
+        join_cols(owned[4 : 4 + hidden_chunks]),
+        join_cols(owned[4 + hidden_chunks :]).T,
+        small[:2],
+        small[2],
+        small[3],
+        small[9:].reshape(-1),
+        small[4],
+        small[5:7],
+        small[7:9],
     )
 
 

time: 1450 us -> 533 us (0.37)
  waiting for transfers between devices: 879 us -> 33.7 us
  blocking collectives: 308 us -> 0 us
  Pallas kernels: 0 us -> 171 us
  local copies, waits for them, and re-layouts: 42.6 us -> 71.5 us
  other arithmetic: 31 us -> 59.7 us
    reduce_scatter x3 -> x0, waiting for transfers between devices: 410 us -> none  [the longest x1 143 us: shards(): lax.psum_scatter(up_weight_gradient, 'fsdp', scatter_dimension=0, tiled=T...]
    unnamed x22 -> x8, waiting for transfers between devices: 368 us -> 0.8 us
    pallas_call x0 -> x2, Pallas kernels: none -> 171 us  [the longest x1 91.3 us: scatter_rows(): pl.pallas_call(partial(scatter_kernel, chunks), name='scatter_rows', out_...]
    unnamed x2 -> x0, blocking collectives: 154 us -> none
    all_gather x4 -> x0, blocking collectives: 151 us -> none  [the longest x1 43.2 us: fetch_params(): lax.all_gather(attention_out_weight, 'fsdp', axis=1, tiled=True)]
    all_gather x3 -> x0, waiting for transfers between devices: 46.7 us -> none  [the longest x1 46.7 us: fetch_params(): lax.all_gather(down_weight, 'fsdp', axis=1, tiled=True)]
    convert_element_type x2, other arithmetic: 0.01 us -> 24.1 us  [the longest x1 17.9 us: shards(): hidden_gradient = gelu_back(d_activated)[0].astype(jnp.bfloat16)]
    slice x0 -> x14, local copies, waits for them, and re-layouts: none -> 19.6 us  [the longest x2 9.45 us: fetch_params(): whole[5:5 + hidden_chunks]]
  transfers between devices with their start and end apart: 18 -> 8, of which waited for: 14 -> 3; matrix products, arithmetic and copies ran while one was open for 11% -> 18% of each run, Pallas kernels for 0% -> 33%
where the time goes in v1:
time: 533 us; the launch traced here: 524 us
  Pallas kernels  171 us (32%)
  matrix products  171 us (32%)
  local copies, waits for them, and re-layouts  71.5 us (13%)
  other arithmetic  59.7 us (11%)
  waiting for transfers between devices  33.7 us (6%)
  between operations  15.1 us (3%)
    pallas_call x1, Pallas kernels, scatter_rows(): pl.pallas_call(partial(scatter_kernel, chunks), name='scatter_rows', out_...  91.3 us
    pallas_call x1, Pallas kernels, gather_rows(): pl.pallas_call(partial(gather_kernel, chunks, 3), name='gather_rows', out...  79.4 us
    dot_general x12, matrix products, attend_back(): jnp.einsum('ij,ie->je', scores_low, rows_grad, preferred_element_type=jnp...  18.9 us
    convert_element_type x1, other arithmetic, shards(): hidden_gradient = gelu_back(d_activated)[0].astype(jnp.bfloat16)  17.9 us
    dot_general x12, matrix products, attend(): jnp.einsum('if,jf->ij', q_feat[begin_row:end_row], k_feat[:end_row], pref...  17.1 us
    dot_general x1, matrix products, run_forward(): jnp.einsum('xwq,qp->xwp', normalized_rows, up_weight, preferred_element_t...  17.1 us
    dot_general x12, matrix products, attend_back(): jnp.einsum('ie,je->ij', rows_grad, values[:end_row], preferred_element_ty...  16.8 us
    dot_general x12, matrix products, attend(): jnp.dot(scores.astype(jnp.bfloat16), values[:end_row], preferred_element_...  15.9 us
  transfers between devices with their start and end apart: 8, of which 3 were waited for; matrix products, arithmetic and copies ran while one was open for 18% of the time, Pallas kernels for 33%

profile of v1, /device:TPU:0, one launch (start us, length us, event | category | flops | bytes accessed | tf_op | source)
XLA Modules:
  0.0 523.6 jit_solution(11386642930880171510)
XLA Ops:
  13.8 79.4 %gather_rows.1 = bf16[13,4,2,2,48,384]{5,4,3,2,1,0:T(8,128)(2,1)S(1)} custom-call(bf16[13,48,384]{2,1,0:T(8,128)(2,1)S(1)} %fusion.113.w_ref), custom_call_target="tpu_custom_call" | custom-call | tf_op jit(solution)/shard_map/gather_rows/pallas_call | solution.py:209
  93.5 2.8 copy-done
  97.9 3.8 bitcast_add_fusion
  109.4 38.2 %while.37 = (s32[]{:T(128)}, f32[6,1024,64]{1,2,0:T(8,128)}, f32[6,1024]{1,0:T(8,128)S(1)}, bf16[6,1024,128]{2,1,0:T(8,128)(2,1)}, bf16[6,1024,128]{2,1,0:T(8,128)(2,1)}, /*index=5*/bf16[6,1024,64]{2,1,0:T(8,128)(2,1)}) while((s32[]{:T(128)}, f32[6,1024,64]{1,2,0:T(8,128)}, f32[6,1024]{1,0:T(8,128)S(1)}, ...), condition=%wide.region_3.4_spmd.clone, body=%wide.region_0.3_spmd.sunk.clone | while | flops 306250240 | bytes 5011033 | solution.py:463
  149.2 2.8 convolution_bitcast_fusion.1
  152.8 9.8 %reduce-scatter.5.cloned.1.call-done = f32[1,512,768]{2,1,0:T(8,128)} async-done(((f32[1,1024,768]{2,1,0:T(8,128)}), f32[1,512,768]{2,1,0:T(8,128)}) %reduce-scatter.5.cloned.1.call-update) | async-done | bytes 1572880 | tf_op jit(solution)/shard_map/reduce_scatter | solution.py:470
  167.3 5.1 fusion.129
  172.4 4.4 copy.103
  176.8 4.3 copy.105
  181.2 17.1 %fusion.55 = (f32[1024,1536]{1,0:T(8,128)S(1)}, f32[1024,1536]{1,0:T(8,128)S(1)}) fusion(f32[1536]{0:T(1024)S(1)} %dynamic-slice_convert_fusion, bf16[768,1536]{0,1:T(8,128)(2,1)} %bitcast.485, bf16[1,1024,768]{2,1,0:T(8,128)(2,1)} %all-gather.7.cloned.1.call-done), kind=kOutput, calls=%fused_computation.81 | convolution fusion | flops 2515009536 | bytes 16521216 | tf_op jit(solution)/shard_map/xwq,qp->xwp/dot_general | solution.py:479
  198.3 2.6 copy-done.1
  202.8 4.3 fusion.86
  207.2 12.2 %reduce-scatter.7.cloned.1.call-done = f32[1,512,768]{2,1,0:T(8,128)} async-done(((f32[1,1024,768]{2,1,0:T(8,128)}), f32[1,512,768]{2,1,0:T(8,128)}) %reduce-scatter.7.cloned.1.call-update) | async-done | bytes 1572880 | tf_op jit(solution)/shard_map/reduce_scatter | solution.py:488
  225.4 10.9 %all-gather.9.cloned.1.call-done = bf16[1,1024,768]{2,1,0:T(8,128)(2,1)} async-done(((bf16[1,512,768]{2,1,0:T(8,128)(2,1)}), bf16[1,1024,768]{2,1,0:T(8,128)(2,1)}) %all-gather.9.cloned.1.call-update) | async-done | bytes 1572880 | tf_op jit(solution)/shard_map/all_gather | solution.py:581
  236.3 12.9 %convert_reduce_fusion = (f32[1536]{0:T(1024)S(1)}, bf16[1024,1536]{1,0:T(8,128)(2,1)S(1)}, f32[1024,1536]{1,0:T(8,128)}) fusion(f32[1024,1536]{1,0:T(8,128)} %copy-done.23, f32[1024,1536]{1,0:T(8,128)} %copy-done.1, f32[1536]{0:T(1024)S(1)} %dynamic-slice_convert_fusion, bf16[768,1536]{0,1:T(8,128)(2,1)} %bitcast.487, ...), kind=kOutput, calls=%fused_computation.99 | convolution fusion | flops 2442656256 | bytes 25964544 | tf_op jit(solution)/shard_map/rcw,ew->rce/dot_general | solution.py:582
  249.2 4.2 convolution_bitcast_fusion
  257.0 17.9 %fusion.63 = (bf16[1536,1024]{0,1:T(8,128)(2,1)}, f32[1536,1024]{0,1:T(8,128)}) fusion(f32[1024,1536]{1,0:T(8,128)} %get-tuple-element.412, f32[1024,1536]{1,0:T(8,128)} %copy-done.1, f32[1536]{0:T(1024)S(1)} %dynamic-slice_convert_fusion), kind=kLoop, calls=%fused_computation.95 | loop fusion | flops 114819072 | bytes 22026240 | tf_op jit(solution)/shard_map/convert_element_type | solution.py:589
  274.8 4.7 copy.133
  284.8 6.2 %fusion.65 = bf16[1536,1024]{0,1:T(8,128)(2,1)S(1)} fusion(f32[1536,1024]{0,1:T(8,128)} %get-tuple-element.366, f32[1024,1536]{1,0:T(8,128)} %copy-done.1, f32[1536]{0:T(1024)S(1)} %dynamic-slice_convert_fusion), kind=kLoop, calls=%fused_computation.98 | loop fusion | flops 6291456 | bytes 15734784 | tf_op jit(solution)/shard_map/convert_element_type | solution.py:482
  291.0 3.1 copy.135
  294.1 6.6 %convolution_convert_fusion.1 = bf16[768,4,384]{2,0,1:T(8,128)(2,1)} fusion(bf16[4,384,1024]{2,1,0:T(8,128)(2,1)} %bitcast.479, bf16[1,1024,768]{2,1,0:T(8,128)(2,1)} %all-gather.7.cloned.1.call-done), kind=kOutput, calls=%fused_computation.141 | convolution fusion | flops 2417098752 | bytes 7077888 | tf_op jit(solution)/shard_map/auf,aub->fb/dot_general | solution.py:596
  300.8 3.2 fusion.94
  304.0 77.0 %while.38 = (s32[]{:T(128)}, f32[6,1024,128]{1,2,0:T(8,128)}, f32[6,1024,128]{1,2,0:T(8,128)}, bf16[6,1024,64]{1,2,0:T(8,128)(2,1)S(1)}, bf16[6,1024,64]{1,2,0:T...) while((s32[]{:T(128)}, f32[6,1024,128]{1,2,0:T(8,128)}, ...), condition=%wide.region_17.18_spmd.clone, body=%wide.region_16.17_spmd.sunk.clone | while | flops 811139584 | bytes 14052473 | solution.py:625
  381.0 5.0 fusion.110
  387.8 3.4 fusion.107
  391.2 5.6 %convolution_convert_fusion = bf16[768,4,384]{2,0,1:T(8,128)(2,1)} fusion(bf16[4,384,1024]{2,1,0:T(8,128)(2,1)S(1)} %bitcast.478, bf16[1,1024,768]{2,1,0:T(8,128)(2,1)} %all-gather.9.cloned.1.call-done), kind=kOutput, calls=%fused_computation.140 | convolution fusion | flops 2417098752 | bytes 7077888 | tf_op jit(solution)/shard_map/job,joe->be/dot_general | solution.py:585
  398.4 2.6 copy.117
  401.0 4.7 convert_bitcast_fusion
  405.7 2.8 copy.116
  408.6 2.6 fusion.109
  411.2 5.3 %pad_maximum_fusion.1.g_ref = bf16[12,4,2,2,48,384]{5,4,3,2,1,0:T(8,128)(2,1)} fusion(bf16[4,4,2,2,48,384]{5,4,3,2,1,0:T(8,128)(2,1)} %bitcast.484, bf16[4,4,2,2,48,384]{5,4,3,2,1,0:T(8,128)(2,1)S(1)} %bitcast.483, bf16[1,4,2,2,48,384]{5,4,3,2,1,0:T(8,128)(2,1)S(1)} %fusion.109, bf16[3,4,2,2,48,384]{5,4,3,2,1,0:T(8,128)(2,1)S(1)} %bitcast.475), kind=kLoop, calls=%fused_computation.80 | loop fusion | flops 10616832 | bytes 14155776 | tf_op jit(solution)/shard_map/concatenate | solution.py:674
  416.4 91.3 %scatter_rows.1 = (f32[12,48,384]{2,1,0:T(8,128)S(1)}, f32[8,128]{1,0:T(8,128)S(1)}) custom-call(bf16[12,4,2,2,48,384]{5,4,3,2,1,0:T(8,128)(2,1)} %pad_maximum_fusion.1.g_ref, f32[4,2,2,8,128]{4,3,2,1,0:T(8,128)S(1)} %bitcast.466), custom_call_target="tpu_custom_call" | custom-call | tf_op jit(solution)/shard_map/scatter_rows/pallas_call | solution.py:235
  (295 shorter events, 166.1 us)
Async XLA Ops:
  7.2 90.7 %all-gather.5.cloned.1.call-start = ((), (), s32[]{:S(2)}) async-start(), calls=%async_computation.4 | async-start | bytes 2359296 | tf_op jit(solution)/shard_map/all_gather | solution.py:438
  7.9 154.8 %reduce-scatter.5.cloned.1.call-start = ((), (), s32[]{:S(2)}) async-start(), calls=%async_computation.5 | async-start | bytes 4718592 | tf_op jit(solution)/shard_map/reduce_scatter | solution.py:470
  93.3 3.0 copy-start
  96.3 5.4 %copy-start.18 = (bf16[3,4,2,2,48,384]{5,4,3,2,1,0:T(8,128)(2,1)}, bf16[3,4,2,2,48,384]{5,4,3,2,1,0:T(8,128)(2,1)S(1)}, u32[]{:S(2)}) copy-start(bf16[3,4,2,2,48,384]{5,4,3,2,1,0:T(8,128)(2,1)S(1)} %slice.319) | copy-start | bytes 5308420
  97.6 4.0 copy-start.21
  101.7 2.4 copy-start.4
  106.2 1.6 copy-start.9
  109.4 39.8 %copy-start.5 = (bf16[1,4,2,2,48,384]{5,4,3,2,1,0:T(8,128)(2,1)S(1)}, bf16[1,4,2,2,48,384]{5,4,3,2,1,0:T(8,128)(2,1)}, u32[]{:S(2)}) copy-start(bf16[1,4,2,2,48,384]{5,4,3,2,1,0:T(8,128)(2,1)} %get-tuple-element.384) | copy-start | bytes 1769476
  149.2 2.8 copy-start.11
  149.2 13.5 %copy-start.8 = (bf16[1,512,768]{2,1,0:T(8,128)(2,1)S(1)}, bf16[1,512,768]{2,1,0:T(8,128)(2,1)}, u32[]{:S(2)}) copy-start(bf16[1,512,768]{2,1,0:T(8,128)(2,1)} %param.29) | copy-start | bytes 2359300
  152.0 29.2 %all-gather.7.cloned.1.call-start = ((), (), s32[]{:S(2)}) async-start(), calls=%async_computation.6 | async-start | bytes 2359296 | tf_op jit(solution)/shard_map/all_gather | solution.py:477
  165.9 53.4 %reduce-scatter.7.cloned.1.call-start = ((), (), s32[]{:S(2)}) async-start(), calls=%async_computation.7 | async-start | bytes 4718592 | tf_op jit(solution)/shard_map/reduce_scatter | solution.py:488
  181.2 21.6 %copy-start.15 = (bf16[4,768,384]{1,2,0:T(8,128)(2,1)S(1)}, bf16[4,768,384]{1,2,0:T(8,128)(2,1)}, u32[]{:S(2)}) copy-start(bf16[4,768,384]{1,2,0:T(8,128)(2,1)} %copy.105) | copy-start | bytes 7077892
  198.3 2.7 copy-start.1
  198.3 4.5 copy-start.23
  207.1 29.2 %all-gather.9.cloned.1.call-start = ((), (), s32[]{:S(2)}) async-start(), calls=%async_computation.8 | async-start | bytes 2359296 | tf_op jit(solution)/shard_map/all_gather | solution.py:581
  219.3 2.4 copy-start.7
  225.2 54.4 %reduce-scatter.9.cloned.1.call-start = ((), (), s32[]{:S(2)}) async-start(), calls=%async_computation.9 | async-start | bytes 4718592 | tf_op jit(solution)/shard_map/reduce_scatter | solution.py:602
  236.3 12.9 %copy-start.14 = (bf16[4,768,384]{1,2,0:T(8,128)(2,1)S(1)}, bf16[4,768,384]{1,2,0:T(8,128)(2,1)}, u32[]{:S(2)}) copy-start(bf16[4,768,384]{1,2,0:T(8,128)(2,1)} %copy.103) | copy-start | bytes 7077892
  253.5 47.2 %all-gather.11.cloned.1.call-start = ((), (), s32[]{:S(2)}) async-start(), calls=%async_computation.10 | async-start | bytes 2359296 | tf_op jit(solution)/shard_map/all_gather | solution.py:609
  282.5 1.2 copy-start.2
  284.8 229.1 %reduce-scatter.11.cloned.1.call-start = ((), (), s32[]{:S(2)}) async-start(), calls=%async_computation.11 | async-start | bytes 2359296 | tf_op jit(solution)/shard_map/reduce_scatter | solution.py:650
  294.1 6.6 %copy-start.20 = (f32[6,1024,64]{1,2,0:T(8,128)S(1)}, f32[6,1024,64]{1,2,0:T(8,128)}, u32[]{:S(2)}) copy-start(f32[6,1024,64]{1,2,0:T(8,128)} %get-tuple-element.263) | copy-start | bytes 4718596
  294.1 6.6 %copy-start.22 = (bf16[384,768]{1,0:T(8,128)(2,1)S(1)}, bf16[384,768]{1,0:T(8,128)(2,1)}, u32[]{:S(2)}) copy-start(bf16[384,768]{1,0:T(8,128)(2,1)} %copy.106) | copy-start | bytes 1769476
  300.8 3.2 copy-start.10
  386.0 1.8 copy-start.19
  386.4 1.4 copy-start.16
  387.8 3.4 copy-start.6
  396.9 4.2 copy-start.17
  405.7 2.9 copy-start.12
  408.6 2.6 copy-start.13
  507.8 6.1 %copy-start.3 = (f32[1,512,768]{2,1,0:T(8,128)S(1)}, f32[1,512,768]{2,1,0:T(8,128)}, u32[]{:S(2)}) copy-start(f32[1,512,768]{2,1,0:T(8,128)} %copy-done.2) | copy-start | bytes 4718596
Sparse Core Ops, SparseCore 0:
  9.6 12.4 all-gather.4
  152.1 10.5 reduce-scatter.4
  166.0 10.9 all-gather.6
  207.2 12.0 reduce-scatter.6
  225.3 10.9 all-gather.8
  253.6 12.0 reduce-scatter.8
  284.9 10.9 all-gather.10
  391.3 10.3 reduce-scatter.10

commit v2 on v0

v2 whole, which is shorter than its diff:
```python
from functools import partial

import jax
import jax.numpy as jnp
import numpy as np
from jax import lax
from jax.experimental import pallas as pl
from jax.experimental.pallas import tpu as pltpu
from jax.sharding import PartitionSpec as P

HEAD_DIM = 64
EPS = 1e-05
MESH = pl.DeviceIdType.MESH
BF16 = jnp.bfloat16
F32 = jnp.float32
TILE = 256
PIECE = 384
SMALL_ROWS = 32
QK_BIAS, VALUE_BIAS, OUT_BIAS, OUT2_BIAS, GAINS, SHIFTS, IN_BIAS = 0, 4, 6, 8, 10, 14, 18
AHEAD = 4


def nn(a, b):
    return jnp.dot(a, b, preferred_element_type=F32)


def nt(a, b):
    return lax.dot_general(a, b, (((1,), (1,)), ((), ())), preferred_element_type=F32)


def tn(a, b):
    return lax.dot_general(a, b, (((0,), (0,)), ((), ())), preferred_element_type=F32)


def place():
    f = lax.axis_index("fsdp")
    return lax.rem(f, 2), lax.rem(f // 2, 2), f // 4, lax.axis_index("tp")


def rank(x, y, z):
    return (z * 2 + y) * 2 + x


def meet(devices):
    barrier = pltpu.get_barrier_semaphore()
    for device in devices:
        pl.semaphore_signal(barrier, inc=1, device_id=device, device_id_type=MESH)
    pl.semaphore_wait(barrier, len(devices))


def remote(source, target, send_sem, recv_sem, device):
    return pltpu.make_async_remote_copy(
        src_ref=source,
        dst_ref=target,
        send_sem=send_sem,
        recv_sem=recv_sem,
        device_id=device,
        device_id_type=MESH,
    )


class Sends:
    def __init__(self):
        self.copies = []

    def start(self, *args):
        copy = remote(*args)
        copy.start()
        self.copies.append(copy)
        return copy

    def settle(self, copies):
        for copy in copies:
            copy.wait_send()
        self.copies = [c for c in self.copies if not any(c is copy for copy in copies)]

    def finish(self):
        self.settle(list(self.copies))


class Gather:
    def __init__(self, pieces, where, send, recv, sends):
        self.pieces, self.send, self.recv, self.sends = pieces, send, recv, sends
        self.x, self.y, self.z, t = where
        x, y, z = self.x, self.y, self.z
        self.z_peers = [(rank(x, y, lax.rem(z + k, 4)), t) for k in (1, 2, 3)]
        self.x_peer, self.y_peer = (rank(1 - x, y, z), t), (rank(x, 1 - y, z), t)
        count = len(pieces)
        self.steps = []
        for step in range(count + 1):
            if step < count:
                self.steps.append(partial(self.second, step))
            if step + AHEAD < count:
                self.steps.append(partial(self.along_z, step + AHEAD))
            if step >= 1:
                self.steps.append(partial(self.third, step - 1))
        self.done_at = {}
        self.at = 0
        self.finished = set()

    def begin(self):
        for piece in range(min(AHEAD, len(self.pieces))):
            self.along_z(piece)

    def view(self, piece, *index):
        _, whole, cols = self.pieces[piece]
        return whole.at[(*index, slice(None), cols)]

    def sems(self, piece, stage):
        return self.send.at[piece, stage], self.recv.at[piece, stage]

    def arrive(self, piece, stage, *index):
        target = self.view(piece, *index)
        remote(target, target, *self.sems(piece, stage), self.x_peer).wait_recv()

    def along_z(self, piece):
        slab, _, cols = self.pieces[piece]
        for k in range(3):
            self.sends.start(
                slab.at[:, cols],
                self.view(piece, self.z, self.y, self.x),
                *self.sems(piece, k),
                self.z_peers[k],
            )

    def second(self, piece):
        for k in range(3):
            self.arrive(piece, k, lax.rem(self.z + 3 - k, 4), self.y, self.x)
        own = self.view(piece, slice(None), self.y, self.x)
        self.sends.start(own, own, *self.sems(piece, 3), self.x_peer if piece % 2 else self.y_peer)

    def third(self, piece):
        if piece % 2:
            self.arrive(piece, 3, slice(None), self.y, 1 - self.x)
            own = self.view(piece, slice(None), self.y, slice(None))
        else:
            self.arrive(piece, 3, slice(None), 1 - self.y, self.x)
            own = self.view(piece, slice(None), slice(None), self.x)
        self.sends.start(own, own, *self.sems(piece, 4), self.y_peer if piece % 2 else self.x_peer)

    def pump(self, count):
        for step in self.steps[self.at : self.at + count]:
            step()
        self.at = min(self.at + count, len(self.steps))

    def need(self, piece):
        while self.at < len(self.steps) and any(
            step.func == self.third and step.args[0] <= piece for step in self.steps[self.at :]
        ):
            self.pump(1)
        for p in range(piece + 1):
            if p not in self.finished:
                self.finished.add(p)
                if p % 2:
                    self.arrive(p, 4, slice(None), 1 - self.y, slice(None))
                else:
                    self.arrive(p, 4, slice(None), slice(None), 1 - self.x)


class Scatter:
    def __init__(self, pieces, where, r1, r2, r3, send, recv, sends):
        self.pieces, self.r1, self.r2, self.r3 = pieces, r1, r2, r3
        self.send, self.recv, self.sends = send, recv, sends
        self.x, self.y, self.z, t = where
        x, y, z = self.x, self.y, self.z
        self.z_peers = [(rank(x, y, lax.rem(z + k, 4)), t) for k in (1, 2, 3)]
        self.x_peer, self.y_peer = (rank(1 - x, y, z), t), (rank(x, 1 - y, z), t)
        self.steps = []
        count = len(pieces)
        self.stage = [0] * count
        self.order = []

    def sems(self, piece, stage):
        return self.send.at[piece, stage], self.recv.at[piece, stage]

    def arrive(self, target, piece, stage):
        remote(target, target, *self.sems(piece, stage), self.x_peer).wait_recv()

    def part(self, piece, *index):
        grads, cols, _ = self.pieces[piece]
        return grads.at[(*index, slice(None), cols)]

    def first(self, piece):
        every = slice(None)
        source = (
            self.part(piece, every, 1 - self.y, every)
            if piece % 2
            else self.part(piece, every, every, 1 - self.x)
        )
        self.sends.start(
            source, self.r1.at[piece], *self.sems(piece, 0), self.y_peer if piece % 2 else self.x_peer
        )
        self.order.append(piece)
        n = len(self.order)
        self.steps.append(partial(self.second, piece))
        if n > 1:
            self.steps.append(partial(self.third, self.order[n - 2]))
        if n > 3:
            self.steps.append(partial(self.last, self.order[n - 4]))

    def second(self, piece):
        self.arrive(self.r1.at[piece], piece, 0)
        grads, cols, _ = self.pieces[piece]
        for q in range(4):
            for r in range(2):
                mine = grads[q, self.y, r, :, cols] if piece % 2 else grads[q, r, self.x, :, cols]
                self.r1[piece, q, r] = (mine.astype(F32) + self.r1[piece, q, r].astype(F32)).astype(BF16)
        other = self.r1.at[piece, :, 1 - self.x] if piece % 2 else self.r1.at[piece, :, 1 - self.y]
        self.sends.start(
            other, self.r2.at[piece], *self.sems(piece, 1), self.x_peer if piece % 2 else self.y_peer
        )

    def third(self, piece):
        self.arrive(self.r2.at[piece], piece, 1)
        for q in range(4):
            mine = self.r1[piece, q, self.x] if piece % 2 else self.r1[piece, q, self.y]
            self.r2[piece, q] = (mine.astype(F32) + self.r2[piece, q].astype(F32)).astype(BF16)
        for k in range(3):
            self.sends.start(
                self.r2.at[piece, lax.rem(self.z + k + 1, 4)],
                self.r3.at[piece, k],
                *self.sems(piece, 2 + k),
                self.z_peers[k],
            )

    def last(self, piece):
        total = self.r2[piece, self.z].astype(F32)
        for k in range(3):
            self.arrive(self.r3.at[piece, k], piece, 2 + k)
            total = total + self.r3[piece, k].astype(F32)
        self.pieces[piece][2](total)

    def pump(self, count):
        for step in self.steps[:count]:
            step()
        self.steps = self.steps[count:]

    def finish(self):
        n = len(self.order)
        self.steps.append(partial(self.third, self.order[n - 1]))
        for k in range(max(n - 3, 0), n):
            self.steps.append(partial(self.last, self.order[k]))
        self.pump(len(self.steps))


def layer_kernel(fused, names, *refs):
    r = dict(zip(names, refs))
    where = x, y, z, t = place()
    partner = (lax.axis_index("fsdp"), 1 - t)
    sends = Sends()
    gy, xs = r["grad_out"], r["inputs"]
    wqkv, wo, wup, wdn = r["wqkv"], r["wo"], r["wup"], r["wdn"]
    gqkv, go, gup, gdn = r["gqkv"], r["go"], r["gup"], r["gdn"]
    X, HB, DF = r["X"], r["HB"], r["DF"]
    DATT = DF
    FQ, FK, VA, SS, DN = r["FQ"], r["FK"], r["VA"], r["SS"], r["DN"]
    DEN, CTX, N1, RS1, DR = r["DEN"], r["CTX"], r["N1"], r["RS1"], r["DR"]
    ACT, GP, DPRE, SB, RB = r["ACT"], r["GP"], r["DPRE"], r["SB"], r["RB"]
    BV, SG, table = r["BV"], r["SG"], r["table"]
    tps, tpr = r["tps"], r["tpr"]
    length, width = X.shape
    local = length // 2
    tiles = local // TILE
    cols = wo.shape[-1]
    hidden = wup.shape[-1]
    pairs = cols // 128
    chunks = length // TILE
    halves = hidden // (2 * PIECE)
    mine, other = t * local, (1 - t) * local

    def rows_at(base, tile):
        return pl.ds(pl.multiple_of(base + tile * TILE, TILE), TILE)

    passed = {}

    def to_partner(source, target, index):
        passed[index] = sends.start(source, target, tps.at[index], tpr.at[index], partner)

    def leave(first):
        sends.settle([passed[first + tile] for tile in range(tiles)])

    def from_partner(target, index):
        remote(target, target, tps.at[index], tpr.at[index], partner).wait_recv()

    def flat(ref, begin=0, size=None):
        size = ref.shape[-1] if size is None else size
        return ref[:, :, :, :, begin : begin + size].reshape(width, size)

    if fused:
        x_peer, y_peer = (rank(1 - x, y, z), t), (rank(x, 1 - y, z), t)
        z_peers = [(rank(x, y, lax.rem(z + k, 4)), t) for k in (1, 2, 3)]
        meet(z_peers + [x_peer, y_peer, partner])
        sl = r["small"]
        span = [slice(k * PIECE, (k + 1) * PIECE) for k in range(max(pairs, 2 * halves))]
        sources = (
            [(sl, r["SM"], span[0])]
            + [(r["sqkv"], wqkv, span[p]) for p in range(pairs)]
            + [(r["so"], wo, span[0])]
            + [(r["sup"], wup, span[k]) for k in range(2 * halves)]
            + [(r["sdn"], wdn, span[k]) for k in range(2 * halves)]
        )
        gather = Gather(sources, where, r["ags"], r["agr"], sends)
        first_up = 2 + pairs
        first_dn = first_up + 2 * halves
        gather.begin()
        own = []
        for k, (slab, whole) in enumerate(
            [(sl, r["SM"]), (r["sqkv"], wqkv), (r["so"], wo), (r["sup"], wup), (r["sdn"], wdn)]
        ):
            own.append(pltpu.make_async_copy(slab, whole.at[z, y, x], r["own"].at[k]))
            own[-1].start()
        pump_in, need = gather.pump, gather.need
    else:
        meet([partner])
        first_up = first_dn = 0
        pump_in = need = lambda count: None

    here = pltpu.make_async_copy(xs.at[0], X.at[pl.ds(mine, local)], r["own"].at[5])
    here.start()
    to_partner(xs.at[0], X.at[pl.ds(mine, local)], 0)
    if fused:
        for copy in own:
            copy.wait()
    here.wait()
    SG[...] = jnp.zeros_like(SG)
    r["SI"][...] = jnp.zeros_like(r["SI"])
    pump_in(1)
    from_partner(X.at[pl.ds(other, local)], 0)

    lane = lax.broadcasted_iota(jnp.int32, (TILE, 128), 1)
    low = lane < 64

    def swap(v):
        return pltpu.roll(v, 64, 1)

    need(0)
    if fused:
        total = jnp.zeros((SMALL_ROWS, PIECE), F32)
        for a in range(4):
            for b in range(2):
                for c in range(2):
                    total = total + r["SM"][a, b, c].astype(F32)
        BV[...] = total
    else:
        BV[...] = r["small"][...]

    def small_row(row):
        return jnp.concatenate([BV[row : row + 1, :], BV[row + 1 : row + 2, :]], 1)

    def own_half(row):
        return jnp.where(t == 0, BV[row : row + 1, :], BV[row + 1 : row + 2, :])

    out_bias, out2_bias = small_row(OUT_BIAS), small_row(OUT2_BIAS)
    gain0, gain1 = small_row(GAINS), small_row(GAINS + 2)
    shift0, shift1 = small_row(SHIFTS), small_row(SHIFTS + 2)
    in_bias = []
    for j in range(halves):
        at = IN_BIAS + 2 * j
        in_bias.append(
            jnp.where(t == 0, small_row(at), small_row(at + 2 * halves))
        )
    bq, bk, bv = own_half(QK_BIAS), own_half(QK_BIAS + 2), own_half(VALUE_BIAS)

    for p in range(pairs):
        need(1 + p)
        at = p * 128

        @pl.loop(0, chunks)
        def _(i):
            rows = rows_at(0, i)
            pre = nn(X[rows, :], flat(wqkv, p * 384, 384))
            cs = table[rows, :]
            q = jnp.maximum(pre[:, :128] + bq[:, at : at + 128], 0.0)
            k = jnp.maximum(pre[:, 128:256] + bk[:, at : at + 128], 0.0)
            v = pre[:, 256:] + bv[:, at : at + 128]
            qs, ks, vs = swap(q), swap(k), swap(v)
            FQ[2 * p, rows, :] = (jnp.where(low, q, qs) * cs).astype(BF16)
            FQ[2 * p + 1, rows, :] = (jnp.where(low, qs, q) * cs).astype(BF16)
            FK[2 * p, rows, :] = (jnp.where(low, k, ks) * cs).astype(BF16)
            FK[2 * p + 1, rows, :] = (jnp.where(low, ks, k) * cs).astype(BF16)
            VA[2 * p, rows, :] = jnp.where(low, v, 1.0).astype(BF16)
            VA[2 * p + 1, rows, :] = jnp.where(low, vs, 1.0).astype(BF16)

        pump_in(1)

        def attend(i, states):
            rows = rows_at(0, i)
            ahead = lax.broadcasted_iota(jnp.int32, (TILE, TILE), 0) >= lax.broadcasted_iota(
                jnp.int32, (TILE, TILE), 1
            )
            both, after = [], []
            for h in range(2):
                q, k, va = FQ[2 * p + h, rows, :], FK[2 * p + h, rows, :], VA[2 * p + h, rows, :]
                before = states[h].astype(BF16)
                SS[2 * p + h, i] = before
                scores = jnp.where(ahead, nt(q, k), 0.0).astype(BF16)
                both.append(nn(scores, va) + nn(q, before))
                after.append(states[h] + tn(k, va))
            num = jnp.where(low, both[0], swap(both[1]))
            den = jnp.where(low, swap(both[0]), both[1])
            DEN[rows, at : at + 128] = den
            CTX[rows, at : at + 128] = (num / jnp.maximum(den, 1.0)).astype(BF16)
            return tuple(after)

        start = (jnp.zeros((128, 128), F32), jnp.zeros((128, 128), F32))
        lax.fori_loop(0, chunks, attend, start)
        pump_in(2)

    need(1 + pairs)
    for tile in range(tiles):
        rows = rows_at(other, tile)
        SB[0, tile] = nt(CTX[rows, :], flat(wo)).astype(BF16)
        to_partner(SB.at[0, tile], RB.at[0, tile], 1 + tile)
    pump_in(1)
    for tile in range(tiles):
        rows, here_rows = rows_at(mine, tile), rows_at(0, tile)
        part = nt(CTX[rows, :], flat(wo))
        from_partner(RB.at[0, tile], 1 + tile)
        resid = X[rows, :].astype(F32) + (part + RB[0, tile].astype(F32) + out_bias)
        center = resid - jnp.mean(resid, -1, keepdims=True)
        rstd = lax.rsqrt(jnp.mean(center * center, -1, keepdims=True) + EPS)
        normed = center * rstd
        N1[here_rows, :] = normed
        RS1[here_rows, :] = jnp.broadcast_to(rstd, (TILE, 128))
        HB[rows, :] = (normed * gain0 + shift0).astype(BF16)
        to_partner(HB.at[rows], HB.at[rows], 3 + tile)
        pump_in(1)

    for j in range(halves):
        need(first_up + 2 * j + 1)
        for half in range(2):
            if j == 0 and half == 1:
                for tile in range(tiles):
                    from_partner(HB.at[rows_at(other, tile)], 3 + tile)
            begin = j * 2 * PIECE

            @pl.loop(0, tiles)
            def _(tile):
                rows = rows_at(other if half else mine, tile)
                u = nn(HB[rows, :], flat(wup, begin, 2 * PIECE)) + in_bias[j]
                cdf = 0.5 * (1.0 + lax.erf(u * np.float32(0.5**0.5)))
                pdf = jnp.exp(-0.5 * u * u) * np.float32((2.0 * np.pi) ** -0.5)
                ACT[rows, begin : begin + 2 * PIECE] = (u * cdf).astype(BF16)
                GP[rows, begin : begin + 2 * PIECE] = (cdf + u * pdf).astype(BF16)

            pump_in(3)

    if fused:
        need(first_dn + 2 * halves - 1)
    for tile in range(tiles):
        rows = rows_at(other, tile)
        SB[1, tile] = nt(ACT[rows, :], flat(wdn)).astype(BF16)
        to_partner(SB.at[1, tile], RB.at[1, tile], 5 + tile)
    sum_df = jnp.zeros((1, width), F32)
    sum_gy, sum_gn = sum_df, sum_df
    for tile in range(tiles):
        rows, here_rows = rows_at(mine, tile), rows_at(0, tile)
        part = nt(ACT[rows, :], flat(wdn))
        from_partner(RB.at[1, tile], 5 + tile)
        h1 = N1[here_rows, :] * gain0 + shift0
        resid = h1 + (part + RB[1, tile].astype(F32)) + out2_bias
        center = resid - jnp.mean(resid, -1, keepdims=True)
        rstd = lax.rsqrt(jnp.mean(center * center, -1, keepdims=True) + EPS)
        normed = center * rstd
        r["output"][0, here_rows, :] = (normed * gain1 + shift1).astype(BF16)
        g = gy[0, here_rows, :].astype(F32)
        sum_gn = sum_gn + jnp.sum(g * normed, 0, keepdims=True)
        sum_gy = sum_gy + jnp.sum(g, 0, keepdims=True)
        e = g * gain1
        back = rstd * (
            e - jnp.mean(e, -1, keepdims=True) - normed * jnp.mean(e * normed, -1, keepdims=True)
        )
        DR[here_rows, :] = back
        low_back = back.astype(BF16)
        sum_df = sum_df + jnp.sum(low_back.astype(F32), 0, keepdims=True)
        DF[rows, :] = low_back
        to_partner(DF.at[rows], DF.at[rows], 7 + tile)

    def keep(row, vector):
        SG[row : row + 1, :] = vector[:, :PIECE]
        SG[row + 1 : row + 2, :] = vector[:, PIECE:]

    keep(OUT2_BIAS, sum_df)
    keep(GAINS + 2, sum_gn)
    keep(SHIFTS + 2, sum_gy)

    if fused:

        def write(name, begin):
            def put(total):
                r[name][:, begin : begin + PIECE] = total

            return put

        def write_qkv(p):
            def put(total):
                for m in range(3):
                    r["oqkv"][m, :, p * 128 : (p + 1) * 128] = total[:, m * 128 : (m + 1) * 128]

            return put

        targets = (
            [(gdn, span[k], write("odn", k * PIECE)) for k in range(2 * halves)]
            + [(gup, span[k], write("oup", k * PIECE)) for k in range(2 * halves)]
            + [(go, span[0], write("oo", 0))]
            + [(gqkv, span[p], write_qkv(p)) for p in range(pairs)]
        )
        scatter = Scatter(targets, where, r["R1"], r["R2"], r["R3"], r["rss"], r["rsr"], sends)
        first_out, pump_out = scatter.first, scatter.pump
    else:
        first_out = pump_out = lambda count: None

    def store(ref, begin, value):
        ref[:, :, :, :, begin : begin + value.shape[1]] = value.astype(BF16).reshape(
            ref.shape[:4] + (value.shape[1],)
        )

    for half in range(2):
        if half == 1:
            for tile in range(tiles):
                from_partner(DF.at[rows_at(other, tile)], 7 + tile)

        @pl.loop(0, tiles)
        def _(tile):
            rows = rows_at(other if half else mine, tile)
            for j in range(halves):
                at = slice(j * 2 * PIECE, (j + 1) * 2 * PIECE)
                dact = nn(DF[rows, :], flat(wdn, j * 2 * PIECE, 2 * PIECE))
                du = (dact * GP[rows, at].astype(F32)).astype(BF16)
                GP[rows, at] = du
                sums = jnp.sum(du.astype(F32), 0, keepdims=True)
                r["SI"][j : j + 1, :] = r["SI"][j : j + 1, :] + sums

    for j in range(halves):
        sums = r["SI"][j : j + 1, :]
        keep(IN_BIAS + 2 * j, jnp.where(t == 0, sums, 0.0))
        keep(IN_BIAS + 2 * halves + 2 * j, jnp.where(t == 0, 0.0, sums))
    for j in range(halves):
        store(gdn, j * 2 * PIECE, tn(DF[...], ACT[:, j * 2 * PIECE : (j + 1) * 2 * PIECE]))
        first_out(2 * j)
        first_out(2 * j + 1)
    leave(1)
    for tile in range(tiles):
        rows = rows_at(other, tile)
        SB[0, tile] = nt(GP[rows, :], flat(wup)).astype(BF16)
        to_partner(SB.at[0, tile], RB.at[0, tile], 9 + tile)
    for j in range(halves):
        store(gup, j * 2 * PIECE, tn(HB[...], GP[:, j * 2 * PIECE : (j + 1) * 2 * PIECE]))
        first_out(2 * halves + 2 * j)
        first_out(2 * halves + 2 * j + 1)

    leave(7)
    sum_da = jnp.zeros((1, width), F32)
    sum_dh, sum_dn = sum_da, sum_da
    for tile in range(tiles):
        rows, here_rows = rows_at(mine, tile), rows_at(0, tile)
        part = nt(GP[rows, :], flat(wup))
        from_partner(RB.at[0, tile], 9 + tile)
        g = DR[here_rows, :] + (part + RB[0, tile].astype(F32))
        normed = N1[here_rows, :]
        sum_dn = sum_dn + jnp.sum(g * normed, 0, keepdims=True)
        sum_dh = sum_dh + jnp.sum(g, 0, keepdims=True)
        e = g * gain0
        rstd = RS1[here_rows, :][:, :1]
        back = rstd * (
            e - jnp.mean(e, -1, keepdims=True) - normed * jnp.mean(e * normed, -1, keepdims=True)
        )
        DR[here_rows, :] = back
        low_back = back.astype(BF16)
        sum_da = sum_da + jnp.sum(low_back.astype(F32), 0, keepdims=True)
        DATT[rows, :] = low_back
        to_partner(DATT.at[rows], DATT.at[rows], 11 + tile)
        pump_out(1)
    keep(OUT_BIAS, sum_da)
    keep(GAINS, sum_dn)
    keep(SHIFTS, sum_dh)

    def project_back(base):
        @pl.loop(0, tiles)
        def _(tile):
            rows = rows_at(base, tile)
            dctx = nn(DATT[rows, :], flat(wo))
            for p in range(pairs):
                at = slice(p * 128, (p + 1) * 128)
                d, den, ctx = dctx[:, at], DEN[rows, at], CTX[rows, at].astype(F32)
                dnum = d / jnp.maximum(den, 1.0)
                product = d * ctx
                shifted = swap(dnum)
                for h in range(2):
                    inside = low if h == 0 else jnp.logical_not(low)
                    total = den[:, h * 64 : h * 64 + 1]
                    dden = -jnp.sum(jnp.where(inside, product, 0.0), -1, keepdims=True) / total
                    dden = jnp.where(total > 1.0, dden, 0.0)
                    high = dden.astype(BF16).astype(F32)
                    rest = jnp.where(lane == 64, high, jnp.where(lane == 65, dden - high, 0.0))
                    DN[2 * p + h, rows, :] = jnp.where(low, shifted if h else dnum, rest).astype(BF16)

    project_back(mine)
    for tile in range(tiles):
        from_partner(DATT.at[rows_at(other, tile)], 11 + tile)
    project_back(other)
    pump_out(1)
    store(go, 0, tn(DATT[...], CTX[...]))
    first_out(4 * halves)
    pump_out(1)

    for p in range(pairs):
        at = p * 384

        def attend_back(step, states):
            i = chunks - 1 - step
            rows = rows_at(0, i)
            cs = table[rows, :]
            ahead = lax.broadcasted_iota(jnp.int32, (TILE, TILE), 0) >= lax.broadcasted_iota(
                jnp.int32, (TILE, TILE), 1
            )
            dqs, dks, dvs, after = [], [], [], []
            for h in range(2):
                q, k, va = FQ[2 * p + h, rows, :], FK[2 * p + h, rows, :], VA[2 * p + h, rows, :]
                dn = DN[2 * p + h, rows, :]
                later = states[h].astype(BF16)
                scores = jnp.where(ahead, nt(q, k), 0.0).astype(BF16)
                dscores = jnp.where(ahead, nt(dn, va), 0.0).astype(BF16)
                dq = (nn(dscores, k) + nt(dn, SS[2 * p + h, i])) * cs
                dk = (tn(dscores, q) + nt(va, later)) * cs
                dvs.append(tn(scores, dn) + nn(k, later))
                dqs.append(dq + swap(dq))
                dks.append(dk + swap(dk))
                after.append(states[h] + tn(q, dn))

            def live(feat):
                a, b = feat[2 * p, rows, :].astype(F32), feat[2 * p + 1, rows, :].astype(F32)
                return jnp.where(low, a, swap(b)) > 0.0

            dq = jnp.where(live(FQ), jnp.where(low, dqs[0], dqs[1]), 0.0)
            dk = jnp.where(live(FK), jnp.where(low, dks[0], dks[1]), 0.0)
            dv = jnp.where(low, dvs[0], swap(dvs[1]))
            dpre = jnp.concatenate([dq, dk, dv], 1).astype(BF16)
            DPRE[rows, at : at + 384] = dpre
            return tuple(after)

        start = (jnp.zeros((128, 128), F32), jnp.zeros((128, 128), F32))
        lax.fori_loop(0, chunks, attend_back, start)
        pump_out(2)
        piece = DPRE[:, at : at + 384]
        store(gqkv, at, tn(X[...], piece))
        first_out(4 * halves + 1 + p)
        sums = jnp.sum(piece.astype(F32), 0, keepdims=True)
        for m, row in enumerate((QK_BIAS, QK_BIAS + 2, VALUE_BIAS)):
            here_sums = sums[:, m * 128 : (m + 1) * 128]
            SG[row : row + 1, p * 128 : (p + 1) * 128] = jnp.where(t == 0, here_sums, 0.0)
            SG[row + 1 : row + 2, p * 128 : (p + 1) * 128] = jnp.where(t == 0, 0.0, here_sums)
        pump_out(2)

    leave(5)
    for tile in range(tiles):
        rows = rows_at(other, tile)
        SB[1, tile] = nt(DPRE[rows, :], flat(wqkv)).astype(BF16)
        to_partner(SB.at[1, tile], RB.at[1, tile], 13 + tile)
    if fused:
        Q, ss, sr = r["Q"], r["sms"], r["smr"]
        sends.start(SG, Q.at[0], ss.at[0], sr.at[0], partner)
        pump_out(2)
        remote(SG, Q.at[0], ss.at[0], sr.at[0], partner).wait_recv()
        Q[1] = SG[...] + Q[0]
        sends.start(Q.at[1], Q.at[2], ss.at[1], sr.at[1], x_peer)
    for tile in range(tiles):
        rows, here_rows = rows_at(mine, tile), rows_at(0, tile)
        part = nt(DPRE[rows, :], flat(wqkv))
        from_partner(RB.at[1, tile], 13 + tile)
        r["grad_input"][0, here_rows, :] = DR[here_rows, :] + (part + RB[1, tile].astype(F32))
        pump_out(1)
    if fused:
        remote(Q.at[2], Q.at[2], ss.at[1], sr.at[1], partner).wait_recv()
        Q[3] = Q[1] + Q[2]
        sends.start(Q.at[3], Q.at[4], ss.at[2], sr.at[2], y_peer)
        pump_out(2)
        remote(Q.at[4], Q.at[4], ss.at[2], sr.at[2], partner).wait_recv()
        Q[5] = Q[3] + Q[4]
        for k in range(3):
            sends.start(Q.at[5], Q.at[6 + k], ss.at[3 + k], sr.at[3 + k], z_peers[k])
        scatter.finish()
        total = Q[5]
        for k in range(3):
            remote(Q.at[6 + k], Q.at[6 + k], ss.at[3 + k], sr.at[3 + k], partner).wait_recv()
            total = total + Q[6 + k]
        r["smalls"][...] = total
    else:
        r["smalls"][...] = SG[...]
    sends.finish()


def layer(fused, inputs, grad_out, slabs, small):
    sqkv, so, sup, sdn = slabs
    _, local, width = inputs.shape
    length, cols, hidden = 2 * local, so.shape[-1], sup.shape[-1]
    heads, chunks, tiles = cols // HEAD_DIM, length // TILE, local // TILE
    part = width // 16
    lead = (4, 2, 2, part)
    angles = np.pi / 2.0 * np.arange(length, dtype=np.float64) / length
    table = np.concatenate(
        [np.repeat(np.cos(angles)[:, None], 64, 1), np.repeat(np.sin(angles)[:, None], 64, 1)], 1
    ).astype(np.float32)
    vmem = pl.BlockSpec(memory_space=pltpu.VMEM)
    hbm = pl.BlockSpec(memory_space=pl.ANY)
    dma = pltpu.SemaphoreType.DMA
    sizes = dict(qkv=3 * cols, o=cols, up=hidden, dn=hidden)
    pieces = (4 * cols + 2 * hidden) // PIECE

    ins = [("inputs", inputs, hbm), ("grad_out", grad_out, vmem), ("table", jnp.asarray(table), vmem)]
    if fused:
        ins += [("sqkv", sqkv, vmem), ("so", so, vmem), ("sup", sup, vmem), ("sdn", sdn, vmem)]
    else:
        wholes = [slab.reshape(lead + slab.shape[-1:]) for slab in slabs]
        ins += [(name, value, vmem) for name, value in zip(("wqkv", "wo", "wup", "wdn"), wholes)]
    ins += [("small", small, vmem)]

    outs = [
        ("output", (1, local, width), BF16),
        ("grad_input", (1, local, width), F32),
        ("smalls", (SMALL_ROWS, PIECE), F32),
    ]
    if fused:
        outs += [
            ("oqkv", (3, part, cols), F32),
            ("oo", (part, cols), F32),
            ("oup", (part, hidden), F32),
            ("odn", (part, hidden), F32),
        ]
    else:
        outs += [("g" + name, lead + (size,), BF16) for name, size in sizes.items()]

    def v(*shape, dtype=BF16):
        return pltpu.VMEM(shape, dtype)

    scratch = dict(
        X=v(length, width),
        HB=v(length, width),
        DF=v(length, width),
        FQ=v(heads, length, 128),
        FK=v(heads, length, 128),
        VA=v(heads, length, 128),
        DN=v(heads, length, 128),
        SS=v(heads, chunks, 128, 128),
        DEN=v(length, cols, dtype=F32),
        CTX=v(length, cols),
        N1=v(local, width, dtype=F32),
        RS1=v(local, 128, dtype=F32),
        DR=v(local, width, dtype=F32),
        ACT=v(length, hidden),
        GP=v(length, hidden),
        DPRE=v(length, 3 * cols),
        SB=v(2, tiles, TILE, width),
        RB=v(2, tiles, TILE, width),
        BV=v(SMALL_ROWS, PIECE, dtype=F32),
        SG=v(SMALL_ROWS, PIECE, dtype=F32),
        SI=v(8, 2 * PIECE, dtype=F32),
        tps=dma((16,)),
        tpr=dma((16,)),
        own=dma((6,)),
    )
    if fused:
        scratch.update({"w" + name: v(*lead, size) for name, size in sizes.items()})
        scratch.update({"g" + name: v(*lead, size) for name, size in sizes.items()})
        scratch.update(
            SM=v(4, 2, 2, SMALL_ROWS, PIECE),
            Q=v(9, SMALL_ROWS, PIECE, dtype=F32),
            R1=v(pieces, 4, 2, part, PIECE),
            R2=v(pieces, 4, part, PIECE),
            R3=v(pieces, 3, part, PIECE),
            ags=dma((pieces + 1, 5)),
            agr=dma((pieces + 1, 5)),
            rss=dma((pieces, 5)),
            rsr=dma((pieces, 5)),
            sms=dma((6,)),
            smr=dma((6,)),
        )
    names = [name for name, _, _ in ins] + [name for name, _, _ in outs] + list(scratch)
    results = pl.pallas_call(
        partial(layer_kernel, fused, names),
        name="layer",
        out_shape=tuple(jax.ShapeDtypeStruct(shape, dtype) for _, shape, dtype in outs),
        in_specs=[spec for _, _, spec in ins],
        out_specs=tuple(vmem for _ in outs),
        scratch_shapes=list(scratch.values()),
        compiler_params=pltpu.CompilerParams(
            collective_id=0, has_side_effects=True, vmem_limit_bytes=64 << 20
        ),
    )(*[value for _, value, _ in ins])
    output, grad_input, smalls, *grads = results
    return output, grad_input, smalls, grads


def shards(
    inputs,
    query_key_value_weight,
    attention_out_weight,
    up_weight,
    down_weight,
    qk_bias,
    value_bias,
    out_bias,
    ffn_in_bias,
    ffn_out_bias,
    norm_gains,
    norm_biases,
    grad_out,
):
    rank_here, ranks = lax.axis_index("fsdp"), lax.axis_size("fsdp")
    _, rows, cols = query_key_value_weight.shape
    pairs = cols // 128
    width = inputs.shape[2]
    fused = ranks == 16 and rows % 16 == 0
    sqkv = query_key_value_weight.reshape(3, rows, pairs, 128)
    sqkv = jnp.transpose(sqkv, (1, 2, 0, 3)).reshape(rows, 3 * cols)
    slabs = (sqkv, attention_out_weight.T, up_weight, down_weight.T)

    at_home = (jnp.arange(ranks) == rank_here).astype(BF16)[None, :, None]
    kinds = jnp.concatenate(
        [qk_bias, value_bias[None], out_bias[None], ffn_out_bias[None], norm_gains, norm_biases], 0
    )
    vectors = (kinds[:, None, :] * at_home).reshape(-1, width)
    inner = (ffn_in_bias[None, None, :] * at_home).reshape(-1, width)
    small = jnp.concatenate([vectors, inner], 0)
    small = jnp.pad(small, ((0, SMALL_ROWS * PIECE // width - small.shape[0]), (0, 0)))
    small = small.reshape(SMALL_ROWS, PIECE)

    if not fused:
        slabs = tuple(lax.all_gather(slab, "fsdp", axis=0, tiled=True) for slab in slabs)
        small = lax.psum(small.astype(F32), "fsdp")
    output, grad_input, smalls, grads = layer(fused, inputs, grad_out, slabs, small)
    if fused:
        dqkv, do, dup, ddn = grads
    else:
        dqkv, do, dup, ddn = [
            lax.psum_scatter(g.reshape(width, -1).astype(F32), "fsdp", scatter_dimension=0, tiled=True)
            for g in grads
        ]
        dqkv = jnp.transpose(dqkv.reshape(rows, pairs, 3, 128), (2, 0, 1, 3)).reshape(3, rows, cols)
        smalls = lax.psum(smalls, ("fsdp", "tp"))
    vectors = smalls.reshape(-1, width)
    mine = lax.dynamic_slice_in_dim(vectors[:9], rank_here * rows, rows, 1)
    inner_rows = ffn_in_bias.shape[0]
    inner = vectors[9 : 9 + inner_rows * ranks // width].reshape(-1)
    return (
        output,
        grad_input,
        dqkv,
        do.T,
        dup,
        ddn.T,
        mine[0:2],
        mine[2],
        mine[3],
        lax.dynamic_slice_in_dim(inner, rank_here * inner_rows, inner_rows, 0),
        mine[4],
        mine[5:7],
        mine[7:9],
    )


def solution(mesh):
    return jax.shard_map(
        shards,
        mesh=mesh,
        in_specs=(
            P("fsdp", "tp", None),
            P(None, "fsdp", "tp"),
            P("tp", "fsdp"),
            P("fsdp", "tp"),
            P("tp", "fsdp"),
            P(None, "fsdp"),
            P("fsdp"),
            P("fsdp"),
            P("fsdp"),
            P("fsdp"),
            P(None, "fsdp"),
            P(None, "fsdp"),
            P("fsdp", "tp", None),
        ),
        out_specs=(
            P("fsdp", "tp", None),
            P("fsdp", "tp", None),
            P(None, "fsdp", "tp"),
            P("tp", "fsdp"),
            P("fsdp", "tp"),
            P("tp", "fsdp"),
            P(None, "fsdp"),
            P("fsdp"),
            P("fsdp"),
            P("fsdp"),
            P("fsdp"),
            P(None, "fsdp"),
            P(None, "fsdp"),
        ),
        check_vma=False,
    )
```

time: 1450 us -> 224 us (0.15)
  waiting for transfers between devices: 879 us -> 0 us
  blocking collectives: 308 us -> 0 us
  Pallas kernels: 0 us -> 208 us
  matrix products: 164 us -> 0 us
  other arithmetic: 31 us -> 0.04 us
  local copies, waits for them, and re-layouts: 42.6 us -> 14.6 us
  between operations: 17.7 us -> 0.74 us
    reduce_scatter x7 -> x0, waiting for transfers between devices: 439 us -> none  [the longest x1 143 us: shards(): lax.psum_scatter(up_weight_gradient, 'fsdp', scatter_dimension=0, tiled=T...]
    unnamed x22 -> x0, waiting for transfers between devices: 368 us -> none
    pallas_call x0 -> x1, Pallas kernels: none -> 208 us  [layer(): pl.pallas_call(partial(layer_kernel, fused, names), name='layer', out_sha...]
    dot_general x84 -> x0, matrix products: 164 us -> none  [the longest x1 19.9 us: run_forward(): jnp.einsum('xwq,qp->xwp', normalized_rows, up_weight, preferred_element_t...]
    unnamed x2 -> x0, blocking collectives: 154 us -> none
    all_gather x4 -> x0, blocking collectives: 151 us -> none  [the longest x1 43.2 us: fetch_params(): lax.all_gather(attention_out_weight, 'fsdp', axis=1, tiled=True)]
    all_gather x7 -> x0, waiting for transfers between devices: 71.2 us -> none  [the longest x1 46.7 us: fetch_params(): lax.all_gather(down_weight, 'fsdp', axis=1, tiled=True)]
    unnamed x68 -> x16, local copies, waits for them, and re-layouts: 21.3 us -> 5.97 us
  transfers between devices with their start and end apart: 18 -> 0, of which waited for: 14 -> 0; matrix products, arithmetic and copies ran while one was open for 11% -> 0% of each run, Pallas kernels for 0% -> 0%
where the time goes in v2:
time: 224 us
  Pallas kernels  208 us (93%)
  local copies, waits for them, and re-layouts  14.6 us (7%)
    pallas_call x1, Pallas kernels, layer(): pl.pallas_call(partial(layer_kernel, fused, names), name='layer', out_sha...  208 us
    unnamed x16, local copies, waits for them, and re-layouts  5.97 us

profile of v2, /device:TPU:0, one launch (start us, length us, event | category | flops | bytes accessed | tf_op | source)
XLA Modules:
  0.0 223.7 jit_solution(17050132832248741400)
XLA Ops:
  0.7 0.7 mul.54
  1.3 0.1 mul.55
  1.4 1.5 concatenate.6
  2.9 0.1 mul.50
  3.0 0.1 mul.51
  3.1 0.1 mul.57
  3.1 0.1 mul.58
  3.3 0.1 mul.49
  3.4 0.6 reshape.66.refs_7_
  4.0 0.9 reshape.64
  5.0 0.1 copy.28
  5.1 0.7 reshape.65.refs_3_
  5.8 208.4 %layer.1 = (bf16[1,512,768]{2,1,0:T(8,128)(2,1)}, f32[1,512,768]{2,1,0:T(8,128)}, f32[32,384]{1,0:T(8,128)}, f32[3,48,384]{2,1,0:T(8,128)}, f32[48,384]{1,0:T(8,...) custom-call(bf16[1,512,768]{2,1,0:T(8,128)(2,1)} %refs_0_.1, bf16[1,512,768]{2,1,0:T(8,128)(2,1)} %refs_1_.1, ...), custom_call_target="tpu_custom_call" | custom-call | tf_op jit(solution)/shard_map/layer/pallas_call | solution.py:779
  214.2 0.0 copy-start
  214.2 0.9 slice.33
  215.1 0.8 slice.28
  215.8 0.6 dynamic_slice.7
  216.5 0.6 dynamic-slice_bitcast_fusion
  217.1 0.6 fusion.3
  217.7 2.1 copy.35
  219.8 0.0 copy-done
  219.8 0.0 copy-start.3
  219.8 0.0 copy-start.1
  219.8 1.1 copy.36
  221.0 0.0 copy-done.3
  221.0 0.7 copy.37
  221.7 0.0 copy-done.4
  221.7 0.6 copy.38
  222.3 0.0 copy-done.2
  222.3 0.7 copy.39
  223.0 0.0 copy-done.1
  223.0 0.7 copy.40
  (9 shorter events, 0.1 us)
Async XLA Ops:
  214.2 5.6 %copy-start = (f32[1,512,768]{2,1,0:T(8,128)S(1)}, f32[1,512,768]{2,1,0:T(8,128)}, u32[]{:S(2)}) copy-start(f32[1,512,768]{2,1,0:T(8,128)} %get-tuple-element.47) | copy-start | bytes 4718596
  219.8 1.2 copy-start.3
  219.8 1.9 copy-start.4
  219.8 2.5 %copy-start.2 = (f32[48,1536]{1,0:T(8,128)S(1)}, f32[48,1536]{1,0:T(8,128)}, u32[]{:S(2)}) copy-start(f32[48,1536]{1,0:T(8,128)} %get-tuple-element.50) | copy-start | bytes 884740
  219.8 3.2 %copy-start.1 = (f32[48,1536]{1,0:T(8,128)S(1)}, f32[48,1536]{1,0:T(8,128)}, u32[]{:S(2)}) copy-start(f32[48,1536]{1,0:T(8,128)} %get-tuple-element.25) | copy-start | bytes 884740
